TPU v7x, 32 devices: a whole 2x2x4 slice. The times are simulated.
32 devices in a mesh: dp: 16 (over z, y, x), mp: 2 (over core).
Axes of the slice: x: 2, y: 2, z: 4, core: 2. Of those that a mesh axis runs over, the one named last changes fastest.
Arguments:
- hidden: bfloat16 [2048, 4096], P('dp', 'mp'), may hold values from -6 to 6
- attended: bfloat16 [2048, 4096], P('dp', 'mp'), may hold values from -6 to 6
- query_cotangent: bfloat16 [2048, 4096], P('dp', 'mp'), may hold values from -1.5 to 1.5
- output_cotangent: bfloat16 [2048, 4096], P('dp', 'mp'), may hold values from -1.5 to 1.5
- query_projection_weight: bfloat16 [4096, 4096], P('dp', 'mp'), may hold values from -0.09375 to 0.09375
- output_projection_weight: bfloat16 [4096, 4096], P('dp', 'mp'), may hold values from -0.09375 to 0.09375
- narrower: bfloat16 [256, 16, 4096], P('dp', None, 'mp'), may hold values from -0.09375 to 0.09375
- widener: bfloat16 [256, 16, 4096], P('dp', None, 'mp'), may hold values from -0.375 to 0.375
- reducer: bfloat16 [256, 16, 4096], P('dp', None, 'mp'), may hold values from -0.09375 to 0.09375
- enlarger: bfloat16 [256, 16, 4096], P('dp', None, 'mp'), may hold values from -0.375 to 0.375
- block_adapter: int32 [512], P('dp'), may hold values from 0 to 255, as said below
- block_fill: int32 [512], P('dp'), may hold values from 1 to 4
Outputs:
- queries: bfloat16 [2048, 4096], P('dp', 'mp')
- projected: bfloat16 [2048, 4096], P('dp', 'mp')
- hidden_state_gradient: bfloat16 [2048, 4096], P('dp', 'mp')
- attention_output_gradient: bfloat16 [2048, 4096], P('dp', 'mp')
- narrower_gradient: float32 [256, 16, 4096], P('dp', None, 'mp')
- widener_gradient: float32 [256, 16, 4096], P('dp', None, 'mp')
- reducer_gradient: float32 [256, 16, 4096], P('dp', None, 'mp')
- enlarger_gradient: float32 [256, 16, 4096], P('dp', None, 'mp')
Inputs may be any that keep to these rules, and one draw needn't show every extreme that they name: `block_adapter`: the owner of adapter e is e // 16. Among the 32 blocks of one group (one index of dp), at most 2 have adapters of one owner, and some owner has exactly 2 blocks in every group.
All inputs are finite; a program needn't handle non-finite values.
Results may differ from a plain program's by a relative error of at most 0.015.
Values may be sent and summed in bfloat16 or wider, within the bound.
A program may use at most 128 MiB of HBM per device.

v0:
```python
import jax
import jax.numpy as jnp
from jax import lax
from jax.sharding import PartitionSpec as P

adapter_scale = 2.0


def expand_slots(adapter_table, blocks):
    return jnp.einsum(
        "ob,brf->orf", adapter_table, blocks, preferred_element_type=jnp.float32
    ).astype(jnp.bfloat16)


def gather_slot_rows(adapter_table, slots):
    gathered = jnp.einsum(
        "ob,orf->brf", adapter_table, slots, preferred_element_type=jnp.float32
    ).astype(jnp.bfloat16)
    return gathered.reshape(gathered.shape[0] * gathered.shape[1], gathered.shape[2])


def pick_factor(slot_hot, factor):
    return jnp.einsum("se,ekf->skf", slot_hot, factor, preferred_element_type=jnp.float32).astype(
        jnp.bfloat16
    )


def lower_rank(blocks, factor):
    return jnp.einsum("srf,skf->srk", blocks, factor, preferred_element_type=jnp.float32)


def raise_rank(ranks, factor):
    lifted_rows = jnp.einsum("srk,skf->srf", ranks, factor, preferred_element_type=jnp.float32)
    return (adapter_scale * lifted_rows).astype(jnp.bfloat16)


def factor_gradient(ranks, blocks, slot_weights):
    per_slot = jnp.einsum("srk,srf->skf", ranks, blocks, preferred_element_type=jnp.float32)
    summed_rows = jnp.einsum(
        "se,skf->ekf",
        slot_weights,
        per_slot,
        preferred_element_type=jnp.float32,
        precision=lax.Precision.HIGHEST,
    )
    return adapter_scale * summed_rows


def transposed(left, right):
    return lax.dot_general(
        left, right, (((1,), (1,)), ((), ())), preferred_element_type=jnp.float32
    )


def on_device(
    hidden,
    attended,
    query_cotangent,
    output_cotangent,
    query_projection_weight,
    output_projection_weight,
    narrower,
    widener,
    reducer,
    enlarger,
    block_adapter,
    block_fill,
):
    tokens = hidden.shape[0]
    group_blocks = block_adapter.shape[0]
    width = tokens // group_blocks
    owners = lax.axis_size("dp")
    capacity = -(-group_blocks // owners)
    per_owner = narrower.shape[0]
    owner_of = block_adapter // per_owner
    later_ids = lax.broadcasted_iota(jnp.int32, (group_blocks, group_blocks), 0)
    earlier_ids = lax.broadcasted_iota(jnp.int32, (group_blocks, group_blocks), 1)
    before = (owner_of[:, None] == owner_of[None, :]) & (earlier_ids < later_ids)
    position = jnp.sum(before.astype(jnp.int32), axis=1)
    slot_of = owner_of * capacity + position
    slot_ids = lax.broadcasted_iota(jnp.int32, (owners * capacity, group_blocks), 0)
    adapter_table = (slot_ids == slot_of[None, :]).astype(jnp.bfloat16)
    local_ids = lax.broadcasted_iota(jnp.int32, (group_blocks, per_owner), 1)
    local_hot = (local_ids == (block_adapter % per_owner)[:, None]).astype(jnp.bfloat16)
    slot_hot = jnp.dot(adapter_table, local_hot, preferred_element_type=jnp.float32).astype(
        jnp.bfloat16
    )
    row_ids = lax.broadcasted_iota(jnp.int32, (group_blocks, width), 1)
    live = (row_ids < block_fill[:, None]).astype(jnp.bfloat16).reshape(tokens, 1)
    query_masked = query_cotangent * live
    output_masked = output_cotangent * live

    def to_blocks(values):
        return values.reshape(group_blocks, width, values.shape[1])

    hid_full, att_full = (
        lax.all_gather(hidden, "mp", axis=1, tiled=True),
        lax.all_gather(attended, "mp", axis=1, tiled=True),
    )
    query_columns, output_columns = (
        lax.all_gather(query_projection_weight, "dp", axis=0, tiled=True),
        lax.all_gather(output_projection_weight, "dp", axis=0, tiled=True),
    )
    query_base_product = jnp.dot(hid_full, query_columns, preferred_element_type=jnp.float32)
    output_base_product = jnp.dot(att_full, output_columns, preferred_element_type=jnp.float32)
    hidden_part = transposed(query_masked, query_columns)
    attended_part = transposed(output_masked, output_columns)
    hidden_total_sum, attended_total_sum = (
        lax.psum_scatter(
            hidden_part.astype(jnp.bfloat16), "mp", scatter_dimension=1, tiled=True
        ).astype(jnp.float32),
        lax.psum_scatter(
            attended_part.astype(jnp.bfloat16), "mp", scatter_dimension=1, tiled=True
        ).astype(jnp.float32),
    )
    hid_send = expand_slots(adapter_table, to_blocks(hidden))
    att_send = expand_slots(adapter_table, to_blocks(attended))
    qcot_send = expand_slots(adapter_table, to_blocks(query_masked))
    ocot_send = expand_slots(adapter_table, to_blocks(output_masked))
    hid_recv, att_recv, qcot_recv, ocot_recv, hot_recv = (
        lax.all_to_all(hid_send, "dp", split_axis=0, concat_axis=0, tiled=True),
        lax.all_to_all(att_send, "dp", split_axis=0, concat_axis=0, tiled=True),
        lax.all_to_all(qcot_send, "dp", split_axis=0, concat_axis=0, tiled=True),
        lax.all_to_all(ocot_send, "dp", split_axis=0, concat_axis=0, tiled=True),
        lax.all_to_all(slot_hot, "dp", split_axis=0, concat_axis=0, tiled=True),
    )
    query_down_factor = pick_factor(hot_recv, narrower)
    query_up_factor = pick_factor(hot_recv, widener)
    output_down_factor = pick_factor(hot_recv, reducer)
    output_up_factor = pick_factor(hot_recv, enlarger)
    query_rank_rows, output_rank_rows, query_backward_pass, output_backward_pass = (
        lax.psum(lower_rank(hid_recv, query_down_factor).astype(jnp.bfloat16), "mp").astype(
            jnp.float32
        ),
        lax.psum(lower_rank(att_recv, output_down_factor).astype(jnp.bfloat16), "mp").astype(
            jnp.float32
        ),
        lax.psum(lower_rank(qcot_recv, query_up_factor).astype(jnp.bfloat16), "mp").astype(
            jnp.float32
        ),
        lax.psum(lower_rank(ocot_recv, output_up_factor).astype(jnp.bfloat16), "mp").astype(
            jnp.float32
        ),
    )
    query_rank_rows = query_rank_rows.astype(jnp.bfloat16)
    output_rank_rows = output_rank_rows.astype(jnp.bfloat16)
    query_backward_pass = query_backward_pass.astype(jnp.bfloat16)
    output_backward_pass = output_backward_pass.astype(jnp.bfloat16)
    query_slot_rows, output_slot_rows, hidden_slot_rows, attended_slot_rows = (
        lax.all_to_all(
            raise_rank(query_rank_rows, query_up_factor),
            "dp",
            split_axis=0,
            concat_axis=0,
            tiled=True,
        ),
        lax.all_to_all(
            raise_rank(output_rank_rows, output_up_factor),
            "dp",
            split_axis=0,
            concat_axis=0,
            tiled=True,
        ),
        lax.all_to_all(
            raise_rank(query_backward_pass, query_down_factor),
            "dp",
            split_axis=0,
            concat_axis=0,
            tiled=True,
        ),
        lax.all_to_all(
            raise_rank(output_backward_pass, output_down_factor),
            "dp",
            split_axis=0,
            concat_axis=0,
            tiled=True,
        ),
    )
    slot_weights = hot_recv.astype(jnp.float32)
    narrower_gradient = factor_gradient(query_backward_pass, hid_recv, slot_weights)
    widener_gradient = factor_gradient(query_rank_rows, qcot_recv, slot_weights)
    reducer_gradient = factor_gradient(output_backward_pass, att_recv, slot_weights)
    enlarger_gradient = factor_gradient(output_rank_rows, ocot_recv, slot_weights)
    query_adapter_term = gather_slot_rows(adapter_table, query_slot_rows)
    output_adapter_term = gather_slot_rows(adapter_table, output_slot_rows)
    hidden_adapter_term = gather_slot_rows(adapter_table, hidden_slot_rows)
    attended_adapter_term = gather_slot_rows(adapter_table, attended_slot_rows)
    queries = (query_base_product + query_adapter_term.astype(jnp.float32)).astype(jnp.bfloat16)
    projected = (output_base_product + output_adapter_term.astype(jnp.float32)).astype(jnp.bfloat16)
    hidden_state_gradient = (hidden_total_sum + hidden_adapter_term.astype(jnp.float32)).astype(
        jnp.bfloat16
    )
    attention_output_gradient = (
        attended_total_sum + attended_adapter_term.astype(jnp.float32)
    ).astype(jnp.bfloat16)
    return (
        queries,
        projected,
        hidden_state_gradient,
        attention_output_gradient,
        narrower_gradient,
        widener_gradient,
        reducer_gradient,
        enlarger_gradient,
    )


def solution(mesh):
    placed = (
        P("dp", "mp"),
        P("dp", "mp"),
        P("dp", "mp"),
        P("dp", "mp"),
        P("dp", "mp"),
        P("dp", "mp"),
        P("dp", None, "mp"),
        P("dp", None, "mp"),
        P("dp", None, "mp"),
        P("dp", None, "mp"),
        P("dp"),
        P("dp"),
    )
    return jax.shard_map(
        on_device,
        mesh=mesh,
        in_specs=placed,
        out_specs=(
            P("dp", "mp"),
            P("dp", "mp"),
            P("dp", "mp"),
            P("dp", "mp"),
            P("dp", None, "mp"),
            P("dp", None, "mp"),
            P("dp", None, "mp"),
            P("dp", None, "mp"),
        ),
        check_vma=False,
    )
```

profile of v0, /device:TPU:0, one launch (start us, length us, event | category | flops | bytes accessed | tf_op | source)
XLA Modules:
  0.0 531.3 jit_solution(1490017530341518138)
XLA Ops:
  9.8 8.3 %all-to-all-start.1 = ((bf16[16,2,16]{2,1,0:T(2,128)(2,1)}), bf16[16,2,16]{2,1,0:T(2,128)(2,1)S(1)}, u32[]{:S(2)}, u32[]{:S(2)}) async-start(bf16[16,2,16]{2,1,0:T(2,128)(2,1)} %bitcast.2), calls=%async_computation.1 | async-start | bytes 16384 | tf_op jit(solution)/shard_map/all_to_all | solution.py:125
  21.2 4.3 all-to-all-done.1
  25.4 3.6 all-to-all-start
  31.2 20.5 %all-to-all-done = bf16[32,4,2048]{2,1,0:T(4,128)(2,1)S(1)} async-done(((bf16[32,4,2048]{2,1,0:T(4,128)(2,1)}), bf16[32,4,2048]{2,1,0:T(4,128)(2,1)S(1)}, u32[]{:S(2)}, u32[]{:S(2)}) %all-to-all-start) | async-done | bytes 524320 | tf_op jit(solution)/shard_map/all_to_all | solution.py:121
  51.7 10.6 %all-to-all-start.3 = ((bf16[32,4,2048]{2,1,0:T(4,128)(2,1)}), bf16[32,4,2048]{2,1,0:T(4,128)(2,1)S(1)}, u32[]{:S(2)}, u32[]{:S(2)}) async-start(bf16[32,4,2048]{2,1,0:T(4,128)(2,1)} %copy.148), calls=%async_computation.3 | async-start | bytes 1048576 | tf_op jit(solution)/shard_map/all_to_all | solution.py:122
  65.6 2.0 convolution_convert_fusion.9
  69.8 14.6 %all-to-all-done.3 = bf16[32,4,2048]{2,1,0:T(4,128)(2,1)S(1)} async-done(((bf16[32,4,2048]{2,1,0:T(4,128)(2,1)}), bf16[32,4,2048]{2,1,0:T(4,128)(2,1)S(1)}, u32[]{:S(2)}, u32[]{:S(2)}) %all-to-all-start.3) | async-done | bytes 524320 | tf_op jit(solution)/shard_map/all_to_all | solution.py:122
  84.4 9.6 %all-to-all-start.5 = ((bf16[32,4,2048]{2,1,0:T(4,128)(2,1)}), bf16[32,4,2048]{2,1,0:T(4,128)(2,1)S(1)}, u32[]{:S(2)}, u32[]{:S(2)}) async-start(bf16[32,4,2048]{2,1,0:T(4,128)(2,1)} %copy.159), calls=%async_computation.6 | async-start | bytes 1048576 | tf_op jit(solution)/shard_map/all_to_all | solution.py:123
  97.1 2.7 convolution_convert_fusion.5
  99.8 2.7 convolution_convert_fusion.3
  102.5 2.7 convolution_convert_fusion.4
  105.1 10.8 %all-to-all-done.5 = bf16[32,4,2048]{2,1,0:T(4,128)(2,1)S(1)} async-done(((bf16[32,4,2048]{2,1,0:T(4,128)(2,1)}), bf16[32,4,2048]{2,1,0:T(4,128)(2,1)S(1)}, u32[]{:S(2)}, u32[]{:S(2)}) %all-to-all-start.5) | async-done | bytes 524320 | tf_op jit(solution)/shard_map/all_to_all | solution.py:123
  115.9 10.5 %all-to-all-start.7 = ((bf16[32,4,2048]{2,1,0:T(4,128)(2,1)}), bf16[32,4,2048]{2,1,0:T(4,128)(2,1)S(1)}, u32[]{:S(2)}, u32[]{:S(2)}) async-start(bf16[32,4,2048]{2,1,0:T(4,128)(2,1)} %copy.166), calls=%async_computation.9 | async-start | bytes 1048576 | tf_op jit(solution)/shard_map/all_to_all | solution.py:124
  126.4 4.0 convolution_convert_fusion.2
  135.0 6.9 %all-to-all-done.7 = bf16[32,4,2048]{2,1,0:T(4,128)(2,1)S(1)} async-done(((bf16[32,4,2048]{2,1,0:T(4,128)(2,1)}), bf16[32,4,2048]{2,1,0:T(4,128)(2,1)S(1)}, u32[]{:S(2)}, u32[]{:S(2)}) %all-to-all-start.7) | async-done | bytes 524320 | tf_op jit(solution)/shard_map/all_to_all | solution.py:124
  141.9 2.9 fusion.51
  144.8 3.9 all-reduce
  148.8 5.3 %fusion.22 = bf16[32,4,2048]{2,1,0:T(4,128)(2,1)} fusion(bf16[32,4,16]{2,1,0:T(4,128)(2,1)S(1)} %get-tuple-element.40, bf16[32,16,2048]{2,0,1:T(8,128)(2,1)} %convolution_convert_fusion.4), kind=kOutput, calls=%fused_computation.26 | convolution fusion | flops 8912896 | bytes 2625536 | tf_op jit(solution)/shard_map/srk,skf->srf/dot_general | solution.py:33
  154.1 5.2 all-to-all-start.2
  159.3 2.7 fusion.88
  162.8 2.8 fusion.90
  165.7 3.2 fusion.23
  168.8 2.8 fusion.89
  171.6 4.0 fusion.8
  175.7 6.6 %all-to-all-done.2 = bf16[32,4,2048]{2,1,0:T(4,128)(2,1)S(1)} async-done(((bf16[32,4,2048]{2,1,0:T(4,128)(2,1)}), bf16[32,4,2048]{2,1,0:T(4,128)(2,1)S(1)}, u32[]{:S(2)}, u32[]{:S(2)}) %all-to-all-start.2) | async-done | bytes 524320 | tf_op jit(solution)/shard_map/all_to_all | solution.py:150
  182.2 10.7 %all-to-all-start.4 = ((bf16[32,4,2048]{2,1,0:T(4,128)(2,1)}), bf16[32,4,2048]{2,1,0:T(4,128)(2,1)S(1)}, u32[]{:S(2)}, u32[]{:S(2)}) async-start(bf16[32,4,2048]{2,1,0:T(4,128)(2,1)} %fusion.23), calls=%async_computation.4 | async-start | bytes 1048576 | tf_op jit(solution)/shard_map/all_to_all | solution.py:157
  193.0 4.8 fusion.24
  197.7 7.5 %fusion.11 = f32[16,16,2048]{2,0,1:T(8,128)} fusion(bf16[32,16,1]{1,0,2:T(8,128)(2,1)S(1)} %bitcast.62, f32[32,16,2048]{2,1,0:T(8,128)} %fusion.88), kind=kOutput, calls=%fused_computation.15 | convolution fusion | flops 201850880 | bytes 6292480 | tf_op jit(solution)/shard_map/se,skf->ekf/dot_general | solution.py:39
  205.2 5.4 %fusion.14 = f32[16,16,2048]{2,0,1:T(8,128)} fusion(bf16[32,16,1]{1,0,2:T(8,128)(2,1)S(1)} %bitcast.63, f32[32,16,2048]{2,1,0:T(8,128)S(1)} %copy-done.2), kind=kOutput, calls=%fused_computation.16 | convolution fusion | flops 201850880 | bytes 6292480 | tf_op jit(solution)/shard_map/se,skf->ekf/dot_general | solution.py:39
  210.6 8.2 %all-to-all-done.4 = bf16[32,4,2048]{2,1,0:T(4,128)(2,1)S(1)} async-done(((bf16[32,4,2048]{2,1,0:T(4,128)(2,1)}), bf16[32,4,2048]{2,1,0:T(4,128)(2,1)S(1)}, u32[]{:S(2)}, u32[]{:S(2)}) %all-to-all-start.4) | async-done | bytes 524320 | tf_op jit(solution)/shard_map/all_to_all | solution.py:157
  218.8 10.3 %all-to-all-start.6 = ((bf16[32,4,2048]{2,1,0:T(4,128)(2,1)}), bf16[32,4,2048]{2,1,0:T(4,128)(2,1)}, u32[]{:S(2)}, u32[]{:S(2)}) async-start(bf16[32,4,2048]{2,1,0:T(4,128)(2,1)} %fusion.24), calls=%async_computation.7 | async-start | bytes 1048576 | tf_op jit(solution)/shard_map/all_to_all | solution.py:164
  229.3 4.8 fusion.25
  234.2 40.2 %all-gather.7.cloned.1.call-done = bf16[4096,2048]{1,0:T(8,128)(2,1)} async-done(((bf16[256,2048]{1,0:T(8,128)(2,1)}), bf16[4096,2048]{1,0:T(8,128)(2,1)}) %all-gather.7.cloned.1.call-update) | async-done | bytes 16777232 | tf_op jit(solution)/shard_map/all_gather | solution.py:101
  274.4 12.4 %convolution_convert_fusion.1 = bf16[128,4096]{1,0:T(8,128)(2,1)} fusion(bf16[128,2048]{1,0:T(8,128)(2,1)S(1)} %copy-done.8, bf16[4096,2048]{1,0:T(8,128)(2,1)} %all-gather.7.cloned.1.call-done), kind=kOutput, calls=%fused_computation.1 | convolution fusion | flops 2148007936 | bytes 18350080 | tf_op jit(solution)/shard_map/dot_general | solution.py:50
  286.8 4.6 all-to-all-start.8
  291.5 6.2 %fusion.17 = f32[16,16,2048]{2,0,1:T(8,128)S(1)} fusion(bf16[32,16,1]{1,0,2:T(8,128)(2,1)S(1)} %bitcast.64, f32[32,16,2048]{2,1,0:T(8,128)} %fusion.90), kind=kOutput, calls=%fused_computation.17 | convolution fusion | flops 201850880 | bytes 6292480 | tf_op jit(solution)/shard_map/se,skf->ekf/dot_general | solution.py:39
  297.7 2.5 copy.179
  300.3 2.5 copy.180
  302.8 2.5 copy.181
  305.3 2.5 copy.182
  318.2 2.6 reshape.72
  324.3 2.8 reshape.73
  327.1 151.2 %all-gather.11.cloned.1.call-done = bf16[4096,2048]{1,0:T(8,128)(2,1)} async-done(((bf16[256,2048]{1,0:T(8,128)(2,1)}), bf16[4096,2048]{1,0:T(8,128)(2,1)}) %all-gather.11.cloned.1.call-update) | async-done | bytes 16777232 | tf_op jit(solution)/shard_map/all_gather | solution.py:102
  478.3 12.4 %convolution_convert_fusion = bf16[128,4096]{1,0:T(8,128)(2,1)} fusion(bf16[128,2048]{1,0:T(8,128)(2,1)S(1)} %copy-done.6, bf16[4096,2048]{1,0:T(8,128)(2,1)} %all-gather.11.cloned.1.call-done), kind=kOutput, calls=%fused_computation | convolution fusion | flops 2148007936 | bytes 18350080 | tf_op jit(solution)/shard_map/dot_general | solution.py:50
  490.8 9.5 %fusion.20 = bf16[128,2048]{1,0:T(8,128)(2,1)} fusion(f32[128,2048]{1,0:T(8,128)S(1)} %reshape.69, bf16[128,4096]{1,0:T(8,128)(2,1)} %all-gather.5.cloned.1.call-done, bf16[4096,2048]{1,0:T(8,128)(2,1)} %all-gather.7.cloned.1.call-done), kind=kOutput, calls=%fused_computation.24 | convolution fusion | flops 2148007936 | bytes 19398656 | tf_op jit(solution)/shard_map/dot_general | solution.py:104
  500.3 9.4 %fusion.21 = bf16[128,2048]{1,0:T(8,128)(2,1)} fusion(f32[128,2048]{1,0:T(8,128)S(1)} %reshape.70, bf16[128,4096]{1,0:T(8,128)(2,1)} %all-gather.9.cloned.1.call-done, bf16[4096,2048]{1,0:T(8,128)(2,1)} %all-gather.11.cloned.1.call-done), kind=kOutput, calls=%fused_computation.25 | convolution fusion | flops 2148007936 | bytes 19398656 | tf_op jit(solution)/shard_map/dot_general | solution.py:105
  510.4 1.9 add_convert_fusion.1
  512.3 9.8 %reduce-scatter.5.cloned.1.call-done = bf16[128,2048]{1,0:T(8,128)(2,1)} async-done(((bf16[128,4096]{1,0:T(8,128)(2,1)}), bf16[128,2048]{1,0:T(8,128)(2,1)}) %reduce-scatter.5.cloned.1.call-update) | async-done | bytes 524304 | tf_op jit(solution)/shard_map/reduce_scatter | solution.py:112
  (99 shorter events, 38.3 us)
Async XLA Ops:
  7.2 89.9 %copy-start = (bf16[16,16,2048]{2,1,0:T(8,128)(2,1)S(1)}, bf16[16,16,2048]{2,1,0:T(8,128)(2,1)}, u32[]{:S(2)}) copy-start(bf16[16,16,2048]{2,1,0:T(8,128)(2,1)} %param.18) | copy-start | bytes 3145732
  7.2 1.5 copy-start.23
  7.2 11.7 %copy-start.15 = (bf16[128,2048]{1,0:T(8,128)(2,1)S(1)}, bf16[128,2048]{1,0:T(8,128)(2,1)}, u32[]{:S(2)}) copy-start(bf16[128,2048]{1,0:T(8,128)(2,1)} %param.12) | copy-start | bytes 1572868
  7.2 267.2 %all-gather.7.cloned.1.call-start = ((), (), s32[]{:S(2)}) async-start(), calls=%async_computation.12 | async-start | bytes 17825792 | tf_op jit(solution)/shard_map/all_gather | solution.py:101
  7.9 470.4 %all-gather.11.cloned.1.call-start = ((), (), s32[]{:S(2)}) async-start(), calls=%async_computation.14 | async-start | bytes 17825792 | tf_op jit(solution)/shard_map/all_gather | solution.py:102
  9.8 15.6 %all-to-all-start.1 = ((bf16[16,2,16]{2,1,0:T(2,128)(2,1)}), bf16[16,2,16]{2,1,0:T(2,128)(2,1)S(1)}, u32[]{:S(2)}, u32[]{:S(2)}) async-start(bf16[16,2,16]{2,1,0:T(2,128)(2,1)} %bitcast.2), calls=%async_computation.1 | async-start | bytes 16384 | tf_op jit(solution)/shard_map/all_to_all | solution.py:125
  18.2 472.6 %all-gather.5.cloned.1.call-start = ((), (), s32[]{:S(2)}) async-start(), calls=%async_computation.11 | async-start | bytes 1572864 | tf_op jit(solution)/shard_map/all_gather | solution.py:97
  18.9 10.1 %copy-start.16 = (bf16[128,2048]{1,0:T(8,128)(2,1)S(1)}, bf16[128,2048]{1,0:T(8,128)(2,1)}, u32[]{:S(2)}) copy-start(bf16[128,2048]{1,0:T(8,128)(2,1)} %param.13) | copy-start | bytes 1572868
  25.4 26.3 %all-to-all-start = ((bf16[32,4,2048]{2,1,0:T(4,128)(2,1)}), bf16[32,4,2048]{2,1,0:T(4,128)(2,1)S(1)}, u32[]{:S(2)}, u32[]{:S(2)}) async-start(bf16[32,4,2048]{2,1,0:T(4,128)(2,1)} %copy.136), calls=%async_computation | async-start | bytes 1048576 | tf_op jit(solution)/shard_map/all_to_all | solution.py:121
  29.2 33.7 %copy-start.22 = (s32[32]{0:T(128)S(1)}, s32[32]{0:T(128)}, u32[]{:S(2)}) copy-start(s32[32]{0:T(128)} %param.23) | copy-start | bytes 388
  51.7 32.7 %all-to-all-start.3 = ((bf16[32,4,2048]{2,1,0:T(4,128)(2,1)}), bf16[32,4,2048]{2,1,0:T(4,128)(2,1)S(1)}, u32[]{:S(2)}, u32[]{:S(2)}) async-start(bf16[32,4,2048]{2,1,0:T(4,128)(2,1)} %copy.148), calls=%async_computation.3 | async-start | bytes 1048576 | tf_op jit(solution)/shard_map/all_to_all | solution.py:122
  62.3 438.0 %all-gather.9.cloned.1.call-start = ((), (), s32[]{:S(2)}) async-start(), calls=%async_computation.13 | async-start | bytes 1572864 | tf_op jit(solution)/shard_map/all_gather | solution.py:98
  64.5 5.3 copy-start.5
  64.5 5.3 copy-start.7
  84.4 31.5 %all-to-all-start.5 = ((bf16[32,4,2048]{2,1,0:T(4,128)(2,1)}), bf16[32,4,2048]{2,1,0:T(4,128)(2,1)S(1)}, u32[]{:S(2)}, u32[]{:S(2)}) async-start(bf16[32,4,2048]{2,1,0:T(4,128)(2,1)} %copy.159), calls=%async_computation.6 | async-start | bytes 1048576 | tf_op jit(solution)/shard_map/all_to_all | solution.py:123
  95.9 3.9 copy-start.20
  99.8 2.7 copy-start.21
  115.9 26.0 %all-to-all-start.7 = ((bf16[32,4,2048]{2,1,0:T(4,128)(2,1)}), bf16[32,4,2048]{2,1,0:T(4,128)(2,1)S(1)}, u32[]{:S(2)}, u32[]{:S(2)}) async-start(bf16[32,4,2048]{2,1,0:T(4,128)(2,1)} %copy.166), calls=%async_computation.9 | async-start | bytes 1048576 | tf_op jit(solution)/shard_map/all_to_all | solution.py:124
  126.4 4.1 copy-start.12
  130.4 1.6 copy-start.11
  132.0 1.6 copy-start.14
  154.1 28.1 %all-to-all-start.2 = ((bf16[32,4,2048]{2,1,0:T(4,128)(2,1)}), bf16[32,4,2048]{2,1,0:T(4,128)(2,1)S(1)}, u32[]{:S(2)}, u32[]{:S(2)}) async-start(bf16[32,4,2048]{2,1,0:T(4,128)(2,1)} %fusion.22), calls=%async_computation.2 | async-start | bytes 1048576 | tf_op jit(solution)/shard_map/all_to_all | solution.py:150
  162.8 2.9 copy-start.13
  182.2 23.0 %copy-start.17 = (bf16[32,4,2048]{2,1,0:T(4,128)(2,1)}, bf16[32,4,2048]{2,1,0:T(4,128)(2,1)S(1)}, u32[]{:S(2)}) copy-start(bf16[32,4,2048]{2,1,0:T(4,128)(2,1)S(1)} %all-to-all-done.2) | copy-start | bytes 1572868
  182.2 36.6 %all-to-all-start.4 = ((bf16[32,4,2048]{2,1,0:T(4,128)(2,1)}), bf16[32,4,2048]{2,1,0:T(4,128)(2,1)S(1)}, u32[]{:S(2)}, u32[]{:S(2)}) async-start(bf16[32,4,2048]{2,1,0:T(4,128)(2,1)} %fusion.23), calls=%async_computation.4 | async-start | bytes 1048576 | tf_op jit(solution)/shard_map/all_to_all | solution.py:157
  197.7 7.5 %copy-start.2 = (f32[32,16,2048]{2,1,0:T(8,128)S(1)}, f32[32,16,2048]{2,1,0:T(8,128)}, u32[]{:S(2)}) copy-start(f32[32,16,2048]{2,1,0:T(8,128)} %fusion.89) | copy-start | bytes 12582916
  210.6 63.8 %copy-start.8 = (bf16[128,2048]{1,0:T(8,128)(2,1)S(1)}, bf16[128,2048]{1,0:T(8,128)(2,1)}, u32[]{:S(2)}) copy-start(bf16[128,2048]{1,0:T(8,128)(2,1)} %copy-done.7) | copy-start | bytes 1572868
  218.8 68.0 %copy-start.19 = (bf16[32,4,2048]{2,1,0:T(4,128)(2,1)}, bf16[32,4,2048]{2,1,0:T(4,128)(2,1)S(1)}, u32[]{:S(2)}) copy-start(bf16[32,4,2048]{2,1,0:T(4,128)(2,1)S(1)} %all-to-all-done.4) | copy-start | bytes 1572868
  218.8 68.0 %all-to-all-start.6 = ((bf16[32,4,2048]{2,1,0:T(4,128)(2,1)}), bf16[32,4,2048]{2,1,0:T(4,128)(2,1)}, u32[]{:S(2)}, u32[]{:S(2)}) async-start(bf16[32,4,2048]{2,1,0:T(4,128)(2,1)} %fusion.24), calls=%async_computation.7 | async-start | bytes 1048576 | tf_op jit(solution)/shard_map/all_to_all | solution.py:164
  229.1 281.3 %reduce-scatter.3.cloned.1.call-start = ((), (), s32[]{:S(2)}) async-start(), calls=%async_computation.15 | async-start | bytes 1572864 | tf_op jit(solution)/shard_map/reduce_scatter | solution.py:109
  286.8 34.0 %all-to-all-start.8 = ((bf16[32,4,2048]{2,1,0:T(4,128)(2,1)}), bf16[32,4,2048]{2,1,0:T(4,128)(2,1)}, u32[]{:S(2)}, u32[]{:S(2)}) async-start(bf16[32,4,2048]{2,1,0:T(4,128)(2,1)} %fusion.25), calls=%async_computation.10 | async-start | bytes 1048576 | tf_op jit(solution)/shard_map/all_to_all | solution.py:171
  291.4 230.7 %reduce-scatter.5.cloned.1.call-start = ((), (), s32[]{:S(2)}) async-start(), calls=%async_computation.16 | async-start | bytes 1572864 | tf_op jit(solution)/shard_map/reduce_scatter | solution.py:112
  297.7 2.6 copy-start.3
  300.2 2.5 copy-start.4
  305.3 2.5 copy-start.18
  322.6 155.7 %copy-start.6 = (bf16[128,2048]{1,0:T(8,128)(2,1)S(1)}, bf16[128,2048]{1,0:T(8,128)(2,1)}, u32[]{:S(2)}) copy-start(bf16[128,2048]{1,0:T(8,128)(2,1)} %copy-done.5) | copy-start | bytes 1572868
  500.3 10.1 %copy-start.9 = (f32[128,2048]{1,0:T(8,128)S(1)}, f32[128,2048]{1,0:T(8,128)}, u32[]{:S(2)}) copy-start(f32[128,2048]{1,0:T(8,128)} %reshape.72) | copy-start | bytes 3145732
  500.3 23.7 %copy-start.1 = (bf16[16,16,2048]{2,1,0:T(8,128)(2,1)S(1)}, bf16[16,16,2048]{2,1,0:T(8,128)(2,1)}, u32[]{:S(2)}) copy-start(bf16[16,16,2048]{2,1,0:T(8,128)(2,1)} %param.18) | copy-start | bytes 3145732
  509.7 12.4 %copy-start.10 = (f32[128,2048]{1,0:T(8,128)S(1)}, f32[128,2048]{1,0:T(8,128)}, u32[]{:S(2)}) copy-start(f32[128,2048]{1,0:T(8,128)} %reshape.73) | copy-start | bytes 3145732
Sparse Core Ops, SparseCore 0:
  10.8 263.5 all-gather.6
  277.2 201.0 all-gather.10
  479.8 7.1 all-gather.4
  488.5 10.1 all-gather.8
  500.8 9.5 reduce-scatter.2
  512.5 9.5 reduce-scatter.4
where the time goes:
time: 541 us; the launch traced here: 531 us
  waiting for transfers between devices  276 us (51%)
  matrix products  125 us (23%)
  starting transfers between devices  73.8 us (14%)
  local copies, waits for them, and re-layouts  31.8 us (6%)
  between operations  14.9 us (3%)
  other arithmetic  5.49 us (1%)
    all_gather x1, waiting for transfers between devices, on_device(): lax.all_gather(output_projection_weight, 'dp', axis=0, tiled=True)  151 us
    all_gather x1, waiting for transfers between devices, on_device(): lax.all_gather(query_projection_weight, 'dp', axis=0, tiled=True)  40.2 us
    dot_general x2, matrix products, transposed(): lax.dot_general(left, right, (((1,), (1,)), ((), ())), preferred_element_...  24.8 us
    dot_general x4, matrix products, factor_gradient(): jnp.einsum('se,skf->ekf', slot_weights, per_slot, preferred_element_type=...  23.1 us
    all_to_all x1, waiting for transfers between devices, on_device(): lax.all_to_all(hid_send, 'dp', split_axis=0, concat_axis=0, tiled=True)  20.5 us
    dot_general x4, matrix products, raise_rank(): jnp.einsum('srk,skf->srf', ranks, factor, preferred_element_type=jnp.floa...  18.1 us
    all_to_all x1, waiting for transfers between devices, on_device(): lax.all_to_all(att_send, 'dp', split_axis=0, concat_axis=0, tiled=True)  14.6 us
    dot_general x4, matrix products, pick_factor(): jnp.einsum('se,ekf->skf', slot_hot, factor, preferred_element_type=jnp.fl...  12.1 us
  transfers between devices with their start and end apart: 15, of which 11 were waited for; matrix products, arithmetic and copies ran while one was open for 30% of the time, Pallas kernels for 0%

commit v1 on v0

v1 whole, which is shorter than its diff:
```python
import jax
import jax.numpy as jnp
from jax import lax
from jax.sharding import Mesh, PartitionSpec as P

adapter_scale = 2.0


def product(left, right, contract):
    return lax.dot_general(
        left, right, ((contract[:1], contract[1:]), ((), ())), preferred_element_type=jnp.float32
    )


def one_hot(condition):
    return condition.astype(jnp.bfloat16)


def iota(shape, dimension):
    return lax.broadcasted_iota(jnp.int32, shape, dimension)


def stacked_columns(values, parts):
    wide = values.shape[1] // parts
    return jnp.concatenate([values[:, i * wide : (i + 1) * wide] for i in range(parts)], axis=0)


def unstacked_columns(values, parts):
    rows = values.shape[0] // parts
    return jnp.concatenate([values[i * rows : (i + 1) * rows] for i in range(parts)], axis=1)


def exchange(values, axis):
    return lax.all_to_all(values, axis, split_axis=0, concat_axis=0, tiled=True)


def on_device(
    hidden,
    attended,
    query_cotangent,
    output_cotangent,
    query_projection_weight,
    output_projection_weight,
    narrower,
    widener,
    reducer,
    enlarger,
    block_adapter,
    block_fill,
):
    dp = ("far", "near")
    far = lax.axis_size("far")
    owners = far * lax.axis_size("near")
    tokens = hidden.shape[0]
    group_blocks = block_adapter.shape[0]
    width = tokens // group_blocks
    capacity = -(-group_blocks // owners)
    per_owner, rank = narrower.shape[:2]
    lanes = -(-per_owner // 128) * 128

    query_rows = lax.all_gather(query_projection_weight, "near", axis=0, tiled=True)
    output_rows = lax.all_gather(output_projection_weight, "near", axis=0, tiled=True)

    row_ids = iota((group_blocks, width), 1)
    live = one_hot(row_ids < block_fill[:, None]).reshape(tokens, 1)
    query_masked = query_cotangent * live
    output_masked = output_cotangent * live

    owner_of = block_adapter // per_owner
    later_ids = iota((group_blocks, group_blocks), 0)
    earlier_ids = iota((group_blocks, group_blocks), 1)
    before = (owner_of[:, None] == owner_of[None, :]) & (earlier_ids < later_ids)
    position = jnp.sum(before.astype(jnp.int32), axis=1)
    slot_of = owner_of * capacity + position
    row_of = (slot_of[:, None] * width + row_ids).reshape(1, tokens)
    table = one_hot(iota((owners * capacity * width, tokens), 0) == row_of)
    local_of = jnp.broadcast_to((block_adapter % per_owner)[:, None], (group_blocks, width))
    local_hot = one_hot(iota((tokens, lanes), 1) == local_of.reshape(tokens, 1))
    sent = jnp.concatenate(
        [
            product(table, part, (1, 0)).astype(jnp.bfloat16)
            for part in (local_hot, hidden, attended, query_masked, output_masked)
        ],
        axis=1,
    )
    received = exchange(sent, dp)
    model, query = hidden.shape[1], attended.shape[1]
    ends = [lanes, lanes + model, lanes + model + query, lanes + model + 2 * query]
    hot, hid, att, qcot, ocot = jnp.split(received, ends, axis=1)

    many = per_owner * rank
    spread = one_hot(iota((lanes, many), 0) == iota((lanes, many), 1) // rank)
    own = product(hot, spread, (1, 0))
    fold = one_hot(iota((many, rank), 0) % rank == iota((many, rank), 1))
    factors = [f.reshape(many, f.shape[2]) for f in (narrower, reducer, widener, enlarger)]
    folded = jnp.concatenate(
        [
            product((product(x, f, (1, 1)) * own).astype(jnp.bfloat16), fold, (1, 0))
            for x, f in zip((hid, att, qcot, ocot), factors)
        ],
        axis=1,
    ).astype(jnp.bfloat16)
    ranks = lax.psum(folded, "mp")
    query_rank, output_rank, query_back, output_back = [
        (product(ranks[:, i * rank : (i + 1) * rank], fold, (1, 1)) * own).astype(jnp.bfloat16)
        for i in range(4)
    ]
    down_query, down_output, up_query, up_output = factors
    returned = exchange(
        jnp.concatenate(
            [
                (adapter_scale * product(r, f, (1, 0))).astype(jnp.bfloat16)
                for r, f in (
                    (query_rank, up_query),
                    (output_rank, up_output),
                    (query_back, down_query),
                    (output_back, down_output),
                )
            ],
            axis=1,
        ),
        dp,
    )

    def gradient(ranks, rows, like):
        return (adapter_scale * product(ranks, rows, (0, 0))).reshape(like.shape)

    narrower_gradient = gradient(query_back, hid, narrower)
    widener_gradient = gradient(query_rank, qcot, widener)
    reducer_gradient = gradient(output_back, att, reducer)
    enlarger_gradient = gradient(output_rank, ocot, enlarger)

    hid_full = lax.all_gather(hidden, "mp", axis=1, tiled=True)
    att_full = lax.all_gather(attended, "mp", axis=1, tiled=True)
    depth = hid_full.shape[1] // far
    inputs = exchange(
        jnp.concatenate(
            [stacked_columns(hid_full, far), stacked_columns(att_full, far)], axis=1
        ),
        "far",
    )
    cotangents = [
        lax.all_gather(masked, "far", axis=0, tiled=True)
        for masked in (query_masked, output_masked)
    ]

    def forward(values, weight):
        part = product(values, weight, (1, 0)).astype(jnp.bfloat16)
        parts = exchange(part, "far").reshape(far, tokens, weight.shape[1])
        return jnp.sum(parts.astype(jnp.float32), axis=0)

    def backward(masked, weight):
        part = product(masked, weight, (1, 1)).astype(jnp.bfloat16)
        whole = unstacked_columns(exchange(part, "far"), far)
        return lax.psum_scatter(whole, "mp", scatter_dimension=1, tiled=True)

    base = [
        forward(inputs[:, :depth], query_rows),
        forward(inputs[:, depth:], output_rows),
        backward(cotangents[0], query_rows).astype(jnp.float32),
        backward(cotangents[1], output_rows).astype(jnp.float32),
    ]
    starts = [query, query + model, query + 2 * model]
    adapter_terms = [product(table, part, (0, 0)) for part in jnp.split(returned, starts, axis=1)]
    queries, projected, hidden_state_gradient, attention_output_gradient = [
        (b + t).astype(jnp.bfloat16) for b, t in zip(base, adapter_terms)
    ]
    return (
        queries,
        projected,
        hidden_state_gradient,
        attention_output_gradient,
        narrower_gradient,
        widener_gradient,
        reducer_gradient,
        enlarger_gradient,
    )


def solution(mesh):
    count = mesh.shape["dp"]
    far = 1
    while far * far < count or count % far:
        far += 1
    split = Mesh(
        mesh.devices.reshape(far, count // far, mesh.shape["mp"]), ("far", "near", "mp")
    )
    dp = ("far", "near")
    rows, factors = P(dp, "mp"), P(dp, None, "mp")
    return jax.shard_map(
        on_device,
        mesh=split,
        in_specs=(rows,) * 6 + (factors,) * 4 + (P(dp),) * 2,
        out_specs=(rows,) * 4 + (factors,) * 4,
        check_vma=False,
    )
```

time: 541 us -> 493 us (0.911)
  matrix products: 125 us -> 51 us
  waiting for transfers between devices: 276 us -> 334 us
  local copies, waits for them, and re-layouts: 31.8 us -> 8.28 us
  starting transfers between devices: 73.8 us -> 51.6 us
  other arithmetic: 5.49 us -> 25.2 us
    all_to_all x9 -> x7, waiting for transfers between devices: 71.9 us -> 163 us  [exchange(): return lax.all_to_all(values, axis, split_axis=0, concat_axis=0, tiled=True)]
    dot_general x33 -> x30, matrix products: 125 us -> 51 us  [product(): lax.dot_general(left, right, ((contract[:1], contract[1:]), ((), ())), pr...]
    all_gather x4 -> x6, waiting for transfers between devices: 191 us -> 169 us  [the longest x2 59.4 us: on_device(): lax.all_gather(masked, 'far', axis=0, tiled=True)]
    all_to_all x9 -> x7, starting transfers between devices: 73.4 us -> 51 us  [exchange(): return lax.all_to_all(values, axis, split_axis=0, concat_axis=0, tiled=True)]
    convert_element_type x14 -> x2, local copies, waits for them, and re-layouts: 18.6 us -> 0.24 us  [the longest x1 0.13 us: on_device(): product(table, part, (1, 0)).astype(jnp.bfloat16)]
    concatenate x0 -> x4, other arithmetic: none -> 16 us  [the longest x1 13.9 us: on_device(): jnp.concatenate([stacked_columns(hid_full, far), stacked_columns(att_full...]
    reduce_scatter x2, waiting for transfers between devices: 10.5 us -> 0.01 us  [backward(): return lax.psum_scatter(whole, 'mp', scatter_dimension=1, tiled=True)]
    unnamed x52 -> x31, local copies, waits for them, and re-layouts: 10.7 us -> 1.78 us
  transfers between devices with their start and end apart: 15 -> 15, of which waited for: 11 -> 9; matrix products, arithmetic and copies ran while one was open for 30% -> 16% of each run, Pallas kernels for 0% -> 0%
where the time goes in v1:
time: 493 us; the launch traced here: 488 us
  waiting for transfers between devices  334 us (68%)
  starting transfers between devices  51.6 us (10%)
  matrix products  51 us (10%)
  other arithmetic  25.2 us (5%)
  between operations  14.5 us (3%)
  local copies, waits for them, and re-layouts  8.28 us (2%)
    all_to_all x7, waiting for transfers between devices, exchange(): return lax.all_to_all(values, axis, split_axis=0, concat_axis=0, tiled=True)  163 us
    all_gather x2, waiting for transfers between devices, on_device(): lax.all_gather(masked, 'far', axis=0, tiled=True)  59.4 us
    all_gather x1, waiting for transfers between devices, on_device(): lax.all_gather(output_projection_weight, 'near', axis=0, tiled=True)  52.7 us
    all_gather x1, waiting for transfers between devices, on_device(): lax.all_gather(query_projection_weight, 'near', axis=0, tiled=True)  51.3 us
    all_to_all x7, starting transfers between devices, exchange(): return lax.all_to_all(values, axis, split_axis=0, concat_axis=0, tiled=True)  51 us
    dot_general x30, matrix products, product(): lax.dot_general(left, right, ((contract[:1], contract[1:]), ((), ())), pr...  51 us
    concatenate x1, other arithmetic, on_device(): jnp.concatenate([stacked_columns(hid_full, far), stacked_columns(att_full...  13.9 us
  transfers between devices with their start and end apart: 15, of which 9 were waited for; matrix products, arithmetic and copies ran while one was open for 16% of the time, Pallas kernels for 0%

profile of v1, /device:TPU:0, one launch (start us, length us, event | category | flops | bytes accessed | tf_op | source)
XLA Modules:
  0.0 488.3 jit_solution(7176359094371279426)
XLA Ops:
  7.2 0.7 all-gather.7.cloned.1.call-update
  8.0 0.7 all-gather.9.cloned.1.call-update
  8.7 0.7 fusion.86
  9.6 2.4 broadcast_multiply_fusion
  15.4 1.3 copy-done.3
  16.8 8.3 %all-to-all-start.2 = ((bf16[16,8,8320]{2,1,0:T(8,128)(2,1)}), bf16[16,8,8320]{2,1,0:T(8,128)(2,1)S(1)}, u32[]{:S(2)}, u32[]{:S(2)}) async-start(bf16[16,8,8320]{2,1,0:T(8,128)(2,1)} %bitcast.73), calls=%async_computation.2 | async-start | bytes 4259840 | tf_op jit(solution)/shard_map/all_to_all | solution.py:34
  25.7 2.1 fusion.93
  27.8 5.3 %all-gather.9.cloned.1.call-done = bf16[128,4096]{1,0:T(8,128)(2,1)} async-done(((bf16[128,2048]{1,0:T(8,128)(2,1)}), bf16[128,4096]{1,0:T(8,128)(2,1)}) %all-gather.9.cloned.1.call-update) | async-done | bytes 1048592 | tf_op jit(solution)/shard_map/all_gather | solution.py:134
  33.1 1.3 fusion.94
  34.5 13.9 %maximum_maximum_fusion = bf16[512,2048]{1,0:T(8,128)(2,1)} fusion(bf16[128,1024]{1,0:T(8,128)(2,1)S(1)} %get-tuple-element.21, bf16[128,1024]{1,0:T(8,128)(2,1)S(1)} %get-tuple-element.22, bf16[128,1024]{1,0:T(8,128)(2,1)S(1)} %get-tuple-element.23, bf16[128,1024]{1,0:T(8,128)(2,1)S(1)} %get-tuple-element.20, bf16[128,1024]{1,0:T(8,128)(2,1)S(1)} %copy-done.9, ...), kind=kLoop, calls=%fused_computation.32 | loop fusion | flops 16777216 | bytes 4194304 | tf_op jit(solution)/shard_map/concatenate | solution.py:137
  48.5 41.4 %all-to-all-done.2 = bf16[16,8,8320]{2,1,0:T(8,128)(2,1)S(1)} async-done(((bf16[16,8,8320]{2,1,0:T(8,128)(2,1)}), bf16[16,8,8320]{2,1,0:T(8,128)(2,1)S(1)}, u32[]{:S(2)}, u32[]{:S(2)}) %all-to-all-start.2) | async-done | bytes 2129952 | tf_op jit(solution)/shard_map/all_to_all | solution.py:34
  89.9 20.2 %all-to-all-start = ((bf16[4,128,2048]{2,1,0:T(8,128)(2,1)}), bf16[4,128,2048]{2,1,0:T(8,128)(2,1)}, u32[]{:S(2)}, u32[]{:S(2)}) async-start(bf16[4,128,2048]{2,1,0:T(8,128)(2,1)} %bitcast.72), calls=%async_computation | async-start | bytes 4194304 | tf_op jit(solution)/shard_map/all_to_all | solution.py:34
  110.0 51.3 %all-gather.11.cloned.1.call-done = bf16[1024,2048]{1,0:T(8,128)(2,1)} async-done(((bf16[256,2048]{1,0:T(8,128)(2,1)}), bf16[1024,2048]{1,0:T(8,128)(2,1)}) %all-gather.11.cloned.1.call-update) | async-done | bytes 4194320 | tf_op jit(solution)/shard_map/all_gather | solution.py:61
  161.3 6.2 %convolution_convert_fusion.7 = bf16[512,1024]{1,0:T(8,128)(2,1)} fusion(bf16[512,2048]{1,0:T(8,128)(2,1)} %all-gather.15.cloned.1.call-done, bf16[1024,2048]{1,0:T(8,128)(2,1)} %all-gather.11.cloned.1.call-done), kind=kOutput, calls=%fused_computation.35 | convolution fusion | flops 2148007936 | bytes 7340032 | tf_op jit(solution)/shard_map/dot_general | solution.py:10
  167.5 4.6 all-to-all-start.5
  172.1 59.4 %all-gather.17.cloned.1.call-done = bf16[512,2048]{1,0:T(8,128)(2,1)} async-done(((bf16[128,2048]{1,0:T(8,128)(2,1)}), bf16[512,2048]{1,0:T(8,128)(2,1)}) %all-gather.17.cloned.1.call-update) | async-done | bytes 2097168 | tf_op jit(solution)/shard_map/all_gather | solution.py:143
  231.5 52.7 %all-gather.13.cloned.1.call-done = bf16[1024,2048]{1,0:T(8,128)(2,1)} async-done(((bf16[256,2048]{1,0:T(8,128)(2,1)}), bf16[1024,2048]{1,0:T(8,128)(2,1)}) %all-gather.13.cloned.1.call-update) | async-done | bytes 4194320 | tf_op jit(solution)/shard_map/all_gather | solution.py:62
  284.2 6.2 %convolution_convert_fusion.6 = bf16[512,1024]{1,0:T(8,128)(2,1)} fusion(bf16[512,2048]{1,0:T(8,128)(2,1)} %all-gather.17.cloned.1.call-done, bf16[1024,2048]{1,0:T(8,128)(2,1)} %all-gather.13.cloned.1.call-done), kind=kOutput, calls=%fused_computation.34 | convolution fusion | flops 2148007936 | bytes 7340032 | tf_op jit(solution)/shard_map/dot_general | solution.py:10
  290.4 4.6 all-to-all-start.6
  295.0 6.2 %convolution_convert_fusion = bf16[512,2048]{1,0:T(8,128)(2,1)} fusion(bf16[1024,2048]{1,0:T(8,128)(2,1)} %all-gather.13.cloned.1.call-done, bf16[512,2048]{1,0:T(8,128)(2,1)} %bitcast.1), kind=kOutput, calls=%fused_computation.2 | convolution fusion | flops 2148532224 | bytes 7340032 | tf_op jit(solution)/shard_map/dot_general | solution.py:10
  301.1 19.5 %all-to-all-done.6 = bf16[4,128,1024]{2,1,0:T(8,128)(2,1)} async-done(((bf16[4,128,1024]{2,1,0:T(8,128)(2,1)}), bf16[4,128,1024]{2,1,0:T(8,128)(2,1)}, u32[]{:S(2)}, u32[]{:S(2)}) %all-to-all-start.6) | async-done | bytes 1048608 | tf_op jit(solution)/shard_map/all_to_all | solution.py:34
  320.6 4.4 all-to-all-start.4
  325.3 1.8 fusion.27
  327.1 0.6 fusion.26
  327.7 1.8 fusion.25
  329.6 6.2 %convolution_convert_fusion.1 = bf16[512,2048]{1,0:T(8,128)(2,1)} fusion(bf16[1024,2048]{1,0:T(8,128)(2,1)} %all-gather.11.cloned.1.call-done, bf16[512,2048]{1,0:T(8,128)(2,1)} %bitcast.1), kind=kOutput, calls=%fused_computation.3 | convolution fusion | flops 2148532224 | bytes 7340032 | tf_op jit(solution)/shard_map/dot_general | solution.py:10
  335.7 37.2 %all-to-all-done.4 = bf16[4,128,2048]{2,1,0:T(8,128)(2,1)} async-done(((bf16[4,128,2048]{2,1,0:T(8,128)(2,1)}), bf16[4,128,2048]{2,1,0:T(8,128)(2,1)}, u32[]{:S(2)}, u32[]{:S(2)}) %all-to-all-start.4) | async-done | bytes 2097184 | tf_op jit(solution)/shard_map/all_to_all | solution.py:34
  372.9 4.5 all-to-all-start.1
  377.4 1.8 fusion.24
  379.2 3.4 psum.7
  385.5 1.6 maximum_bitcast_fusion
  387.1 38.1 %all-to-all-done.1 = bf16[4,128,2048]{2,1,0:T(8,128)(2,1)} async-done(((bf16[4,128,2048]{2,1,0:T(8,128)(2,1)}), bf16[4,128,2048]{2,1,0:T(8,128)(2,1)}, u32[]{:S(2)}, u32[]{:S(2)}) %all-to-all-start.1) | async-done | bytes 2097184 | tf_op jit(solution)/shard_map/all_to_all | solution.py:34
  425.2 4.4 all-to-all-start.3
  429.7 1.3 slice_bitcast_fusion.3
  431.0 1.0 pad_maximum_fusion.1
  432.3 1.8 convolution_multiply_fusion.1
  434.1 1.3 slice_bitcast_fusion.7
  435.4 1.0 pad_maximum_fusion
  436.5 1.8 convolution_multiply_fusion.3
  438.2 1.8 convolution_multiply_fusion
  440.0 1.8 convolution_multiply_fusion.2
  441.8 2.1 convert_reduce_fusion
  443.9 2.1 convert_reduce_fusion.1
  446.0 26.5 %all-to-all-done.3 = bf16[16,8,8192]{2,1,0:T(8,128)(2,1)} async-done(((bf16[16,8,8192]{2,1,0:T(8,128)(2,1)}), bf16[16,8,8192]{2,1,0:T(8,128)(2,1)}, u32[]{:S(2)}, u32[]{:S(2)}) %all-to-all-start.3) | async-done | bytes 2097184 | tf_op jit(solution)/shard_map/all_to_all | solution.py:34
  472.5 2.2 fusion.5
  474.6 2.2 fusion.4
  476.8 2.3 fusion.7
  479.2 2.3 fusion.6
  (78 shorter events, 7.6 us)
Async XLA Ops:
  7.2 320.0 %copy-start = (bf16[16,16,2048]{2,1,0:T(8,128)(2,1)S(1)}, bf16[16,16,2048]{2,1,0:T(8,128)(2,1)}, u32[]{:S(2)}) copy-start(bf16[16,16,2048]{2,1,0:T(8,128)(2,1)} %param.19) | copy-start | bytes 3145732
  7.2 18.5 %all-gather.7.cloned.1.call-start = ((), (), s32[]{:S(2)}) async-start(), calls=%async_computation.9 | async-start | bytes 1572864 | tf_op jit(solution)/shard_map/all_gather | solution.py:133
  7.9 25.2 %all-gather.9.cloned.1.call-start = ((), (), s32[]{:S(2)}) async-start(), calls=%async_computation.10 | async-start | bytes 1572864 | tf_op jit(solution)/shard_map/all_gather | solution.py:134
  8.7 4.5 copy-start.14
  8.7 101.4 %all-gather.15.cloned.1.call-start = ((), (), s32[]{:S(2)}) async-start(), calls=%async_computation.13 | async-start | bytes 2621440 | tf_op jit(solution)/shard_map/all_gather | solution.py:143
  9.6 4.6 copy-start.4
  11.9 2.5 copy-start.5
  11.9 2.8 copy-start.2
  12.0 149.4 %all-gather.11.cloned.1.call-start = ((), (), s32[]{:S(2)}) async-start(), calls=%async_computation.11 | async-start | bytes 5242880 | tf_op jit(solution)/shard_map/all_gather | solution.py:61
  12.5 2.5 copy-start.1
  12.6 218.9 %all-gather.17.cloned.1.call-start = ((), (), s32[]{:S(2)}) async-start(), calls=%async_computation.15 | async-start | bytes 2621440 | tf_op jit(solution)/shard_map/all_gather | solution.py:143
  15.4 1.4 copy-start.3
  16.8 73.1 %all-to-all-start.2 = ((bf16[16,8,8320]{2,1,0:T(8,128)(2,1)}), bf16[16,8,8320]{2,1,0:T(8,128)(2,1)S(1)}, u32[]{:S(2)}, u32[]{:S(2)}) async-start(bf16[16,8,8320]{2,1,0:T(8,128)(2,1)} %bitcast.73), calls=%async_computation.2 | async-start | bytes 4259840 | tf_op jit(solution)/shard_map/all_to_all | solution.py:34
  25.1 259.1 %all-gather.13.cloned.1.call-start = ((), (), s32[]{:S(2)}) async-start(), calls=%async_computation.12 | async-start | bytes 5242880 | tf_op jit(solution)/shard_map/all_gather | solution.py:62
  33.1 1.3 copy-start.9
  33.1 1.4 copy-start.10
  33.1 1.4 copy-start.11
  89.9 77.6 %all-to-all-start = ((bf16[4,128,2048]{2,1,0:T(8,128)(2,1)}), bf16[4,128,2048]{2,1,0:T(8,128)(2,1)}, u32[]{:S(2)}, u32[]{:S(2)}) async-start(bf16[4,128,2048]{2,1,0:T(8,128)(2,1)} %bitcast.72), calls=%async_computation | async-start | bytes 4194304 | tf_op jit(solution)/shard_map/all_to_all | solution.py:34
  167.5 122.9 %all-to-all-start.5 = ((bf16[4,128,1024]{2,1,0:T(8,128)(2,1)}), bf16[4,128,1024]{2,1,0:T(8,128)(2,1)}, u32[]{:S(2)}, u32[]{:S(2)}) async-start(bf16[4,128,1024]{2,1,0:T(8,128)(2,1)} %bitcast.86), calls=%async_computation.5 | async-start | bytes 2097152 | tf_op jit(solution)/shard_map/all_to_all | solution.py:34
  290.4 30.3 %all-to-all-start.6 = ((bf16[4,128,1024]{2,1,0:T(8,128)(2,1)}), bf16[4,128,1024]{2,1,0:T(8,128)(2,1)}, u32[]{:S(2)}, u32[]{:S(2)}) async-start(bf16[4,128,1024]{2,1,0:T(8,128)(2,1)} %bitcast.87), calls=%async_computation.7 | async-start | bytes 2097152 | tf_op jit(solution)/shard_map/all_to_all | solution.py:34
  320.6 52.3 %all-to-all-start.4 = ((bf16[4,128,2048]{2,1,0:T(8,128)(2,1)}), bf16[4,128,2048]{2,1,0:T(8,128)(2,1)}, u32[]{:S(2)}, u32[]{:S(2)}) async-start(bf16[4,128,2048]{2,1,0:T(8,128)(2,1)} %bitcast.79), calls=%async_computation.4 | async-start | bytes 4194304 | tf_op jit(solution)/shard_map/all_to_all | solution.py:34
  372.9 52.3 %all-to-all-start.1 = ((bf16[4,128,2048]{2,1,0:T(8,128)(2,1)}), bf16[4,128,2048]{2,1,0:T(8,128)(2,1)}, u32[]{:S(2)}, u32[]{:S(2)}) async-start(bf16[4,128,2048]{2,1,0:T(8,128)(2,1)} %bitcast.78), calls=%async_computation.1 | async-start | bytes 4194304 | tf_op jit(solution)/shard_map/all_to_all | solution.py:34
  382.6 1.6 copy-start.6
  382.6 2.0 copy-start.7
  382.9 2.0 copy-start.12
  383.9 1.3 copy-start.8
  425.2 47.3 %all-to-all-start.3 = ((bf16[16,8,8192]{2,1,0:T(8,128)(2,1)}), bf16[16,8,8192]{2,1,0:T(8,128)(2,1)}, u32[]{:S(2)}, u32[]{:S(2)}) async-start(bf16[16,8,8192]{2,1,0:T(8,128)(2,1)} %maximum_bitcast_fusion), calls=%async_computation.3 | async-start | bytes 4194304 | tf_op jit(solution)/shard_map/all_to_all | solution.py:34
  429.6 2.7 copy-start.13
  429.6 47.2 %reduce-scatter.5.cloned.1.call-start = ((), (), s32[]{:S(2)}) async-start(), calls=%async_computation.16 | async-start | bytes 1572864 | tf_op jit(solution)/shard_map/reduce_scatter | solution.py:155
  432.1 47.1 %reduce-scatter.3.cloned.1.call-start = ((), (), s32[]{:S(2)}) async-start(), calls=%async_computation.14 | async-start | bytes 1572864 | tf_op jit(solution)/shard_map/reduce_scatter | solution.py:155
Sparse Core Ops, SparseCore 0:
  9.5 11.7 all-gather.6
  22.9 10.1 all-gather.8
  35.2 72.7 all-gather.14
  109.7 51.5 all-gather.10
  163.3 68.1 all-gather.16
  233.2 50.9 all-gather.12
  432.7 9.5 reduce-scatter.4
  444.5 9.5 reduce-scatter.2

commit v2 on v1

--- a/solution.py
+++ b/solution.py
@@ -1,6 +1,8 @@
 import jax
 import jax.numpy as jnp
 from jax import lax
+from jax.experimental import pallas as pl
+from jax.experimental.pallas import tpu as pltpu
 from jax.sharding import Mesh, PartitionSpec as P
 
 adapter_scale = 2.0
@@ -20,18 +22,175 @@
     return lax.broadcasted_iota(jnp.int32, shape, dimension)
 
 
-def stacked_columns(values, parts):
-    wide = values.shape[1] // parts
-    return jnp.concatenate([values[:, i * wide : (i + 1) * wide] for i in range(parts)], axis=0)
-
-
-def unstacked_columns(values, parts):
-    rows = values.shape[0] // parts
-    return jnp.concatenate([values[i * rows : (i + 1) * rows] for i in range(parts)], axis=1)
-
-
-def exchange(values, axis):
-    return lax.all_to_all(values, axis, split_axis=0, concat_axis=0, tiled=True)
+def block(ref, index, rows):
+    return ref.at[pl.ds(pl.multiple_of(index * rows, rows), rows)]
+
+
+class Place:
+    def __init__(self):
+        self.far, self.near, self.mp = [lax.axis_index(n) for n in ("far", "near", "mp")]
+        self.fars, self.nears, self.mps = [lax.axis_size(n) for n in ("far", "near", "mp")]
+        self.owner = self.far * self.nears + self.near
+        self.owners = self.fars * self.nears
+
+    def near_peers(self):
+        for step in range(self.nears):
+            near = lax.rem(self.near + step, self.nears)
+            yield near, (self.far, near, self.mp), step == 0
+
+    def far_peers(self):
+        for step in range(self.fars):
+            far = lax.rem(self.far + step, self.fars)
+            yield far, (far, self.near, self.mp), step == 0
+
+    def owner_peers(self):
+        for step in range(self.owners):
+            owner = lax.rem(self.owner + step, self.owners)
+            yield owner, (owner // self.nears, lax.rem(owner, self.nears), self.mp), step == 0
+
+    def skips(self, lane):
+        own_half = self.far // (self.fars // self.mps) == self.mp
+        return jnp.logical_and(own_half, self.far == lane)
+
+    def greet(self):
+        others = [device for _, device, own in self.owner_peers() if not own]
+        for shift in range(1, self.mps):
+            mp = lax.rem(self.mp + shift, self.mps)
+            others += [(far, self.near, mp) for far in range(self.fars)]
+        barrier = pltpu.get_barrier_semaphore()
+        for device in others:
+            pl.semaphore_signal(
+                barrier, inc=1, device_id=device, device_id_type=pl.DeviceIdType.MESH
+            )
+        pl.semaphore_wait(barrier, len(others))
+
+
+def both(condition, remote, local):
+    if condition is True:
+        local()
+    elif condition is False:
+        remote()
+    else:
+        pl.when(jnp.logical_not(condition))(remote)
+        pl.when(condition)(local)
+
+
+def transfer(plan, arrays, out_shapes, chunks, sends, collective_id):
+    count, groups = len(arrays), len(chunks)
+
+    def kernel(*refs):
+        ins, outs = refs[:count], refs[count : count + groups]
+        held = refs[count + groups : count + 2 * groups]
+        send_sem, recv_sem, own_sem = refs[count + 2 * groups :]
+        place = Place()
+        place.greet()
+        routes = list(plan(place, ins, outs))
+
+        def remote(at, landing):
+            _, source, target, device = routes[at][:4]
+            return pltpu.make_async_remote_copy(
+                src_ref=source,
+                dst_ref=target,
+                send_sem=send_sem.at[at],
+                recv_sem=recv_sem.at[landing],
+                device_id=device,
+                device_id_type=pl.DeviceIdType.MESH,
+            )
+
+        def inward(at):
+            group, source = routes[at][:2]
+            return pltpu.make_async_copy(source, held[group], own_sem.at[group])
+
+        def outward(at):
+            group, _, target = routes[at][:3]
+            return pltpu.make_async_copy(held[group], target, own_sem.at[group])
+
+        def nothing():
+            pass
+
+        members = {}
+        for at, route in enumerate(routes):
+            members.setdefault(route[0], []).append(at)
+        for at, (group, _, _, _, own, lane, _) in enumerate(routes):
+            group_routes = members[group]
+            stride = group_routes[-1] - group_routes[-2]
+            landing = at if lane is None else group_routes[0] + lane * stride
+            both(own, lambda: remote(at, landing).start(), lambda: inward(at).start())
+        for at, route in enumerate(routes):
+
+            def pass_on():
+                inward(at).wait()
+                outward(at).start()
+
+            both(route[4], nothing, pass_on)
+        for at, (_, _, _, _, own, _, absent) in enumerate(routes):
+            both(own, lambda: remote(at, at).wait_send(), lambda: outward(at).wait())
+            both(absent, lambda: remote(at, at).wait_recv(), nothing)
+
+    anywhere = pl.BlockSpec(memory_space=pl.ANY)
+    return pl.pallas_call(
+        kernel,
+        out_shape=[jax.ShapeDtypeStruct(shape, jnp.bfloat16) for shape in out_shapes],
+        in_specs=[anywhere] * count,
+        out_specs=[anywhere] * groups,
+        scratch_shapes=[pltpu.VMEM(shape, jnp.bfloat16) for shape in chunks]
+        + [pltpu.SemaphoreType.DMA((sends,))] * 2
+        + [pltpu.SemaphoreType.DMA((groups,))],
+        compiler_params=pltpu.CompilerParams(
+            collective_id=collective_id, has_side_effects=True
+        ),
+    )(*arrays)
+
+
+def distribute(place, ins, outs):
+    slots, first, second, hidden, attended, query, output = ins
+    tokens, rows = hidden.shape[0], first.shape[0]
+    depth = outs[3].shape[1]
+    each = place.fars // place.mps
+    for near, device, own in place.near_peers():
+        for group, weight in ((1, first), (2, second)):
+            yield group, weight, block(outs[group], place.near, rows), device, own, None, own
+    for shift in range(place.mps):
+        mp = lax.rem(place.mp + shift, place.mps)
+        for at in range(each):
+            far = place.mp * each + at
+            own = False if shift else far == place.far
+            absent = place.skips(shift * each + at)
+            for group, values in ((3, hidden), (4, attended)):
+                columns = values.at[:, pl.ds(at * depth, depth)]
+                target = block(outs[group], place.far, tokens)
+                device = (far, place.near, mp)
+                yield group, columns, target, device, own, place.far, absent
+    for far, device, own in place.far_peers():
+        for group, values in ((5, query), (6, output)):
+            target = block(outs[group], place.far, tokens)
+            yield group, values, target, device, own, None, own
+    for owner, device, own in place.owner_peers():
+        yield 0, slots.at[owner], outs[0].at[place.owner], device, own, None, own
+
+
+def collect(place, ins, outs):
+    slots, query, output, hidden, attended = ins
+    tokens = query.shape[0] // place.fars
+    depth = hidden.shape[1]
+    each = place.fars // place.mps
+    for far, device, own in place.far_peers():
+        for group, values in ((1, query), (2, output)):
+            target = block(outs[group], place.far, tokens)
+            yield group, block(values, far, tokens), target, device, own, None, own
+    mp, at = place.far // each, lax.rem(place.far, each)
+    for step, (far, _, own) in enumerate(place.far_peers()):
+        absent = place.skips(step)
+        mine = mp == place.mp if own else False
+        for group, values in ((3, hidden), (4, attended)):
+            target = outs[group].at[
+                pl.ds(pl.multiple_of(place.mp * tokens, tokens), tokens),
+                pl.ds(pl.multiple_of(at * depth, depth), depth),
+            ]
+            device, lane = (far, place.near, mp), place.mp * each + at
+            yield group, block(values, far, tokens), target, device, mine, lane, absent
+    for owner, device, own in place.owner_peers():
+        yield 0, slots.at[owner], outs[0].at[place.owner], device, own, None, own
 
 
 def on_device(
@@ -48,7 +207,6 @@
     block_adapter,
     block_fill,
 ):
-    dp = ("far", "near")
     far = lax.axis_size("far")
     owners = far * lax.axis_size("near")
     tokens = hidden.shape[0]
@@ -57,9 +215,6 @@
     capacity = -(-group_blocks // owners)
     per_owner, rank = narrower.shape[:2]
     lanes = -(-per_owner // 128) * 128
-
-    query_rows = lax.all_gather(query_projection_weight, "near", axis=0, tiled=True)
-    output_rows = lax.all_gather(output_projection_weight, "near", axis=0, tiled=True)
 
     row_ids = iota((group_blocks, width), 1)
     live = one_hot(row_ids < block_fill[:, None]).reshape(tokens, 1)
@@ -83,9 +238,47 @@
         ],
         axis=1,
     )
-    received = exchange(sent, dp)
     model, query = hidden.shape[1], attended.shape[1]
     ends = [lanes, lanes + model, lanes + model + query, lanes + model + 2 * query]
+    near, mps = lax.axis_size("near"), lax.axis_size("mp")
+    depth = model * mps // far
+    depth_out = query * mps // far
+    high, wide = query_projection_weight.shape
+    high_out, wide_out = output_projection_weight.shape
+    slots = (owners, capacity * width, sent.shape[1])
+    received, query_rows, output_rows, inputs, inputs_out, qcots, ocots = transfer(
+        distribute,
+        (
+            sent.reshape(slots),
+            query_projection_weight,
+            output_projection_weight,
+            hidden,
+            attended,
+            query_masked,
+            output_masked,
+        ),
+        (
+            slots,
+            (near * high, wide),
+            (near * high_out, wide_out),
+            (far * tokens, depth),
+            (far * tokens, depth_out),
+            (far * tokens, wide),
+            (far * tokens, wide_out),
+        ),
+        (
+            slots[1:],
+            (high, wide),
+            (high_out, wide_out),
+            (tokens, depth),
+            (tokens, depth_out),
+            (tokens, wide),
+            (tokens, wide_out),
+        ),
+        2 * near + 4 * far + owners,
+        0,
+    )
+    received = received.reshape(sent.shape)
     hot, hid, att, qcot, ocot = jnp.split(received, ends, axis=1)
 
     many = per_owner * rank
@@ -106,20 +299,17 @@
         for i in range(4)
     ]
     down_query, down_output, up_query, up_output = factors
-    returned = exchange(
-        jnp.concatenate(
-            [
-                (adapter_scale * product(r, f, (1, 0))).astype(jnp.bfloat16)
-                for r, f in (
-                    (query_rank, up_query),
-                    (output_rank, up_output),
-                    (query_back, down_query),
-                    (output_back, down_output),
-                )
-            ],
-            axis=1,
-        ),
-        dp,
+    lifted = jnp.concatenate(
+        [
+            (adapter_scale * product(r, f, (1, 0))).astype(jnp.bfloat16)
+            for r, f in (
+                (query_rank, up_query),
+                (output_rank, up_output),
+                (query_back, down_query),
+                (output_back, down_output),
+            )
+        ],
+        axis=1,
     )
 
     def gradient(ranks, rows, like):
@@ -130,35 +320,40 @@
     reducer_gradient = gradient(output_back, att, reducer)
     enlarger_gradient = gradient(output_rank, ocot, enlarger)
 
-    hid_full = lax.all_gather(hidden, "mp", axis=1, tiled=True)
-    att_full = lax.all_gather(attended, "mp", axis=1, tiled=True)
-    depth = hid_full.shape[1] // far
-    inputs = exchange(
-        jnp.concatenate(
-            [stacked_columns(hid_full, far), stacked_columns(att_full, far)], axis=1
-        ),
-        "far",
-    )
-    cotangents = [
-        lax.all_gather(masked, "far", axis=0, tiled=True)
-        for masked in (query_masked, output_masked)
+    parts = [
+        product(values, weight, contract).astype(jnp.bfloat16)
+        for values, weight, contract in (
+            (inputs, query_rows, (1, 0)),
+            (inputs_out, output_rows, (1, 0)),
+            (qcots, query_rows, (1, 1)),
+            (ocots, output_rows, (1, 1)),
+        )
     ]
-
-    def forward(values, weight):
-        part = product(values, weight, (1, 0)).astype(jnp.bfloat16)
-        parts = exchange(part, "far").reshape(far, tokens, weight.shape[1])
-        return jnp.sum(parts.astype(jnp.float32), axis=0)
-
-    def backward(masked, weight):
-        part = product(masked, weight, (1, 1)).astype(jnp.bfloat16)
-        whole = unstacked_columns(exchange(part, "far"), far)
-        return lax.psum_scatter(whole, "mp", scatter_dimension=1, tiled=True)
-
+    slots = (owners, capacity * width, lifted.shape[1])
+    returned, *terms = transfer(
+        collect,
+        (lifted.reshape(slots), *parts),
+        (
+            slots,
+            (far * tokens, wide),
+            (far * tokens, wide_out),
+            (mps * tokens, model),
+            (mps * tokens, query),
+        ),
+        (
+            slots[1:],
+            (tokens, wide),
+            (tokens, wide_out),
+            (tokens, depth),
+            (tokens, depth_out),
+        ),
+        4 * far + owners,
+        1,
+    )
+    returned = returned.reshape(lifted.shape)
     base = [
-        forward(inputs[:, :depth], query_rows),
-        forward(inputs[:, depth:], output_rows),
-        backward(cotangents[0], query_rows).astype(jnp.float32),
-        backward(cotangents[1], output_rows).astype(jnp.float32),
+        jnp.sum(term.reshape(-1, tokens, term.shape[1]).astype(jnp.float32), axis=0)
+        for term in terms
     ]
     starts = [query, query + model, query + 2 * model]
     adapter_terms = [product(table, part, (0, 0)) for part in jnp.split(returned, starts, axis=1)]
@@ -180,7 +375,7 @@
 def solution(mesh):
     count = mesh.shape["dp"]
     far = 1
-    while far * far < count or count % far:
+    while far * far < count or count % far or far % mesh.shape["mp"]:
         far += 1
     split = Mesh(
         mesh.devices.reshape(far, count // far, mesh.shape["mp"]), ("far", "near", "mp")

time: 493 us -> 434 us (0.88)
  the two profiles are of different devices: /device:TPU:0 before, /device:TPU:14 now
where the time goes in v2:
time: 434 us; the launch traced here: 433 us
  Pallas kernels  376 us (87%)
  matrix products  41.3 us (10%)
  other arithmetic  7.55 us (2%)
  local copies, waits for them, and re-layouts  4.49 us (1%)
    pallas_call x2, Pallas kernels, transfer(): pl.pallas_call(kernel, out_shape=[jax.ShapeDtypeStruct(shape, jnp.bfloat1...  376 us
    dot_general x30, matrix products, product(): lax.dot_general(left, right, ((contract[:1], contract[1:]), ((), ())), pr...  41.3 us

profile of v2, /device:TPU:14, one launch (start us, length us, event | category | flops | bytes accessed | tf_op | source)
XLA Modules:
  0.0 433.2 jit_solution(14620078061635097237)
XLA Ops:
  0.7 1.3 copy-done
  2.0 0.7 and_select_fusion.1
  2.7 0.2 convert_reduce_fusion.4
  2.9 0.7 fusion.84
  3.6 0.1 reshape.117
  4.1 0.3 convolution_convert_fusion.8
  4.4 0.1 copy.22
  4.5 1.3 broadcast_multiply_fusion
  5.9 0.7 constant_dynamic-update-slice_fusion
  6.6 1.1 fusion.11
  7.7 1.1 fusion.10
  8.8 1.1 fusion.9
  9.9 1.1 fusion.8
  11.1 187.9 %shard_map.179 = (bf16[16,8,8320]{2,1,0:T(8,128)(2,1)}, bf16[1024,2048]{1,0:T(8,128)(2,1)}, bf16[1024,2048]{1,0:T(8,128)(2,1)}, bf16[512,1024]{1,0:T(8,128)(2,1)...) custom-call(bf16[16,8,8320]{2,1,0:T(8,128)(2,1)} %bitcast.refs_0_, ...), custom_call_target="tpu_custom_call" | custom-call | tf_op jit(solution)/shard_map/pallas_call | solution.py:131
  198.9 1.1 fusion.44
  200.0 2.0 fusion.27
  202.0 1.7 fusion.26
  203.7 1.8 fusion.25
  205.5 1.8 fusion.24
  207.3 3.4 psum.7
  210.7 0.3 fusion.19
  211.0 0.3 fusion.18
  211.4 0.3 fusion.17
  211.7 0.3 fusion.16
  212.0 0.3 fusion
  212.3 0.3 fusion.1
  212.7 0.3 fusion.2
  213.0 0.3 copy-done.10
  213.3 0.3 fusion.3
  213.6 1.5 maximum_bitcast_fusion.refs_0_
  215.1 1.6 copy-done.16
  216.7 3.3 convolution_convert_fusion.7.refs_3_
  220.1 3.7 convolution_convert_fusion.1.refs_1_
  223.7 3.4 convolution_convert_fusion.6.refs_4_
  227.1 3.7 convolution_convert_fusion.refs_2_
  230.7 187.7 %shard_map.180 = (bf16[16,8,8192]{2,1,0:T(8,128)(2,1)}, bf16[512,2048]{1,0:T(8,128)(2,1)}, bf16[512,2048]{1,0:T(8,128)(2,1)}, bf16[256,2048]{1,0:T(8,128)(2,1)}, bf16[256,2048]{1,0:T(8,128)(2,1)}) custom-call(bf16[16,8,8192]{2,1,0:T(8,128)(2,1)} %maximum_bitcast_fusion.refs_0_, bf16[512,2048]{1,0:T(8,128)(2,1)} %convolution_convert_fusion.1.refs_1_, ...), custom_call_target="tpu_custom_call" | custom-call | tf_op jit(solution)/shard_map/pallas_call | solution.py:131
  418.5 2.2 convert_reduce_fusion.1
  420.7 1.1 fusion.4
  421.9 0.4 convert_reduce_fusion
  422.3 1.1 fusion.5
  423.4 0.2 convert_reduce_fusion.3
  423.6 1.1 fusion.6
  424.8 0.2 convert_reduce_fusion.2
  424.9 1.1 fusion.7
  426.1 1.8 convolution_multiply_fusion.1
  427.9 1.8 convolution_multiply_fusion.3
  429.6 1.8 convolution_multiply_fusion
  431.4 1.8 convolution_multiply_fusion.2
  (49 shorter events, 0.5 us)
Async XLA Ops:
  0.6 1.4 copy-start
  0.6 7.0 %copy-start.7 = (bf16[128,2048]{1,0:T(8,128)(2,1)S(1)}, bf16[128,2048]{1,0:T(8,128)(2,1)}, u32[]{:S(2)}) copy-start(bf16[128,2048]{1,0:T(8,128)(2,1)} %refs_4_.1) | copy-start | bytes 1572868
  0.7 5.9 %copy-start.6 = (bf16[128,2048]{1,0:T(8,128)(2,1)S(1)}, bf16[128,2048]{1,0:T(8,128)(2,1)}, u32[]{:S(2)}) copy-start(bf16[128,2048]{1,0:T(8,128)(2,1)} %refs_3_.1) | copy-start | bytes 1572868
  5.9 5.2 %copy-start.1 = (bf16[128,2048]{1,0:T(8,128)(2,1)}, bf16[128,2048]{1,0:T(8,128)(2,1)S(1)}, u32[]{:S(2)}) copy-start(bf16[128,2048]{1,0:T(8,128)(2,1)S(1)} %get-tuple-element.32.refs_6_) | copy-start | bytes 1572868
  5.9 5.2 %copy-start.2 = (bf16[128,2048]{1,0:T(8,128)(2,1)}, bf16[128,2048]{1,0:T(8,128)(2,1)S(1)}, u32[]{:S(2)}) copy-start(bf16[128,2048]{1,0:T(8,128)(2,1)S(1)} %get-tuple-element.33.refs_5_) | copy-start | bytes 1572868
  198.9 4.7 %copy-start.3 = (bf16[16,8,8320]{2,1,0:T(8,128)(2,1)S(1)}, bf16[16,8,8320]{2,1,0:T(8,128)(2,1)}, u32[]{:S(2)}) copy-start(bf16[16,8,8320]{2,1,0:T(8,128)(2,1)} %get-tuple-element.20) | copy-start | bytes 6389764
  210.7 1.6 copy-start.8
  210.7 2.0 copy-start.9
  211.0 2.0 copy-start.13
  212.0 1.3 copy-start.10
  212.7 2.5 copy-start.18
  213.6 3.1 copy-start.16
  216.7 3.3 copy-start.20
  220.0 3.7 copy-start.15
  220.1 3.7 copy-start.17
  223.7 3.4 copy-start.19
  418.4 2.3 copy-start.4
  418.4 3.4 copy-start.5
  421.9 1.5 copy-start.12
  423.4 1.3 copy-start.11
  424.8 1.3 copy-start.14

commit v3 on v2

--- a/solution.py
+++ b/solution.py
@@ -28,35 +28,45 @@
 
 class Place:
     def __init__(self):
-        self.far, self.near, self.mp = [lax.axis_index(n) for n in ("far", "near", "mp")]
-        self.fars, self.nears, self.mps = [lax.axis_size(n) for n in ("far", "near", "mp")]
-        self.owner = self.far * self.nears + self.near
+        names = ("top", "far", "low", "mp")
+        self.top, self.far, self.low, self.mp = [lax.axis_index(name) for name in names]
+        self.tops, self.fars, self.lows, self.mps = [lax.axis_size(name) for name in names]
+        self.near, self.nears = self.top * self.lows + self.low, self.tops * self.lows
+        self.owner = (self.top * self.fars + self.far) * self.lows + self.low
         self.owners = self.fars * self.nears
 
     def near_peers(self):
         for step in range(self.nears):
             near = lax.rem(self.near + step, self.nears)
-            yield near, (self.far, near, self.mp), step == 0
+            device = (near // self.lows, self.far, lax.rem(near, self.lows), self.mp)
+            yield near, device, step == 0
 
     def far_peers(self):
         for step in range(self.fars):
             far = lax.rem(self.far + step, self.fars)
-            yield far, (far, self.near, self.mp), step == 0
+            yield far, (self.top, far, self.low, self.mp), step == 0
 
     def owner_peers(self):
         for step in range(self.owners):
             owner = lax.rem(self.owner + step, self.owners)
-            yield owner, (owner // self.nears, lax.rem(owner, self.nears), self.mp), step == 0
-
-    def skips(self, lane):
-        own_half = self.far // (self.fars // self.mps) == self.mp
-        return jnp.logical_and(own_half, self.far == lane)
+            rest = owner // self.lows
+            top, far, low = rest // self.fars, lax.rem(rest, self.fars), lax.rem(owner, self.lows)
+            yield owner, (top, far, low, self.mp), step == 0
+
+    def feature_peers(self):
+        each = self.tops // self.mps
+        for far, _, own in self.far_peers():
+            for shift in range(self.mps):
+                mp = lax.rem(self.mp + shift, self.mps)
+                for at in range(each):
+                    device = (self.top, far, self.low, mp)
+                    yield far, mp, at, device, own and shift == 0
 
     def greet(self):
         others = [device for _, device, own in self.owner_peers() if not own]
         for shift in range(1, self.mps):
             mp = lax.rem(self.mp + shift, self.mps)
-            others += [(far, self.near, mp) for far in range(self.fars)]
+            others += [(self.top, far, self.low, mp) for far in range(self.fars)]
         barrier = pltpu.get_barrier_semaphore()
         for device in others:
             pl.semaphore_signal(
@@ -65,14 +75,8 @@
         pl.semaphore_wait(barrier, len(others))
 
 
-def both(condition, remote, local):
-    if condition is True:
-        local()
-    elif condition is False:
-        remote()
-    else:
-        pl.when(jnp.logical_not(condition))(remote)
-        pl.when(condition)(local)
+def columns_of(ref, rows, start, columns):
+    return ref.at[rows, pl.ds(pl.multiple_of(start, columns), columns)]
 
 
 def transfer(plan, arrays, out_shapes, chunks, sends, collective_id):
@@ -86,46 +90,36 @@
         place.greet()
         routes = list(plan(place, ins, outs))
 
-        def remote(at, landing):
-            _, source, target, device = routes[at][:4]
-            return pltpu.make_async_remote_copy(
-                src_ref=source,
-                dst_ref=target,
-                send_sem=send_sem.at[at],
-                recv_sem=recv_sem.at[landing],
-                device_id=device,
-                device_id_type=pl.DeviceIdType.MESH,
+        owned = [0] * groups
+        copies, passing = [], []
+        for at, (group, source, target, device, own) in enumerate(routes):
+            if own:
+                keep, sem = held[group].at[owned[group]], own_sem.at[len(passing)]
+                owned[group] += 1
+                inward = pltpu.make_async_copy(source, keep, sem)
+                passing.append((inward, pltpu.make_async_copy(keep, target, sem)))
+                continue
+            copies.append(
+                pltpu.make_async_remote_copy(
+                    src_ref=source,
+                    dst_ref=target,
+                    send_sem=send_sem.at[at],
+                    recv_sem=recv_sem.at[at],
+                    device_id=device,
+                    device_id_type=pl.DeviceIdType.MESH,
+                )
             )
-
-        def inward(at):
-            group, source = routes[at][:2]
-            return pltpu.make_async_copy(source, held[group], own_sem.at[group])
-
-        def outward(at):
-            group, _, target = routes[at][:3]
-            return pltpu.make_async_copy(held[group], target, own_sem.at[group])
-
-        def nothing():
-            pass
-
-        members = {}
-        for at, route in enumerate(routes):
-            members.setdefault(route[0], []).append(at)
-        for at, (group, _, _, _, own, lane, _) in enumerate(routes):
-            group_routes = members[group]
-            stride = group_routes[-1] - group_routes[-2]
-            landing = at if lane is None else group_routes[0] + lane * stride
-            both(own, lambda: remote(at, landing).start(), lambda: inward(at).start())
-        for at, route in enumerate(routes):
-
-            def pass_on():
-                inward(at).wait()
-                outward(at).start()
-
-            both(route[4], nothing, pass_on)
-        for at, (_, _, _, _, own, _, absent) in enumerate(routes):
-            both(own, lambda: remote(at, at).wait_send(), lambda: outward(at).wait())
-            both(absent, lambda: remote(at, at).wait_recv(), nothing)
+        for copy in copies:
+            copy.start()
+        for inward, _ in passing:
+            inward.start()
+        for inward, outward in passing:
+            inward.wait()
+            outward.start()
+        for _, outward in passing:
+            outward.wait()
+        for copy in copies:
+            copy.wait()
 
     anywhere = pl.BlockSpec(memory_space=pl.ANY)
     return pl.pallas_call(
@@ -135,7 +129,7 @@
         out_specs=[anywhere] * groups,
         scratch_shapes=[pltpu.VMEM(shape, jnp.bfloat16) for shape in chunks]
         + [pltpu.SemaphoreType.DMA((sends,))] * 2
-        + [pltpu.SemaphoreType.DMA((groups,))],
+        + [pltpu.SemaphoreType.DMA((sum(shape[0] for shape in chunks),))],
         compiler_params=pltpu.CompilerParams(
             collective_id=collective_id, has_side_effects=True
         ),
@@ -144,53 +138,44 @@
 
 def distribute(place, ins, outs):
     slots, first, second, hidden, attended, query, output = ins
-    tokens, rows = hidden.shape[0], first.shape[0]
-    depth = outs[3].shape[1]
-    each = place.fars // place.mps
+    tokens = hidden.shape[0]
+    each = place.tops // place.mps
     for near, device, own in place.near_peers():
         for group, weight in ((1, first), (2, second)):
-            yield group, weight, block(outs[group], place.near, rows), device, own, None, own
-    for shift in range(place.mps):
-        mp = lax.rem(place.mp + shift, place.mps)
-        for at in range(each):
-            far = place.mp * each + at
-            own = False if shift else far == place.far
-            absent = place.skips(shift * each + at)
-            for group, values in ((3, hidden), (4, attended)):
-                columns = values.at[:, pl.ds(at * depth, depth)]
-                target = block(outs[group], place.far, tokens)
-                device = (far, place.near, mp)
-                yield group, columns, target, device, own, place.far, absent
+            rows = weight.shape[0]
+            yield group, weight, block(outs[group], place.near, rows), device, own
+    for far, mp, at, device, own in place.feature_peers():
+        for group, values in ((3, hidden), (4, attended)):
+            high = outs[group].shape[1] // place.tops
+            source = columns_of(values, slice(None), (at * place.fars + far) * high, high)
+            rows = pl.ds(pl.multiple_of(place.far * tokens, tokens), tokens)
+            target = columns_of(outs[group], rows, (place.mp * each + at) * high, high)
+            yield group, source, target, device, own
     for far, device, own in place.far_peers():
         for group, values in ((5, query), (6, output)):
-            target = block(outs[group], place.far, tokens)
-            yield group, values, target, device, own, None, own
+            yield group, values, block(outs[group], place.far, tokens), device, own
     for owner, device, own in place.owner_peers():
-        yield 0, slots.at[owner], outs[0].at[place.owner], device, own, None, own
+        yield 0, slots.at[owner], outs[0].at[place.owner], device, own
 
 
 def collect(place, ins, outs):
     slots, query, output, hidden, attended = ins
     tokens = query.shape[0] // place.fars
-    depth = hidden.shape[1]
-    each = place.fars // place.mps
+    each = place.tops // place.mps
     for far, device, own in place.far_peers():
         for group, values in ((1, query), (2, output)):
             target = block(outs[group], place.far, tokens)
-            yield group, block(values, far, tokens), target, device, own, None, own
-    mp, at = place.far // each, lax.rem(place.far, each)
-    for step, (far, _, own) in enumerate(place.far_peers()):
-        absent = place.skips(step)
-        mine = mp == place.mp if own else False
+            yield group, block(values, far, tokens), target, device, own
+    for far, mp, at, device, own in place.feature_peers():
         for group, values in ((3, hidden), (4, attended)):
-            target = outs[group].at[
-                pl.ds(pl.multiple_of(place.mp * tokens, tokens), tokens),
-                pl.ds(pl.multiple_of(at * depth, depth), depth),
-            ]
-            device, lane = (far, place.near, mp), place.mp * each + at
-            yield group, block(values, far, tokens), target, device, mine, lane, absent
+            high = values.shape[1] // place.tops
+            rows = pl.ds(pl.multiple_of(far * tokens, tokens), tokens)
+            source = columns_of(values, rows, (mp * each + at) * high, high)
+            rows = pl.ds(pl.multiple_of(place.mp * tokens, tokens), tokens)
+            target = columns_of(outs[group], rows, (at * place.fars + place.far) * high, high)
+            yield group, source, target, device, own
     for owner, device, own in place.owner_peers():
-        yield 0, slots.at[owner], outs[0].at[place.owner], device, own, None, own
+        yield 0, slots.at[owner], outs[0].at[place.owner], device, own
 
 
 def on_device(
@@ -208,7 +193,7 @@
     block_fill,
 ):
     far = lax.axis_size("far")
-    owners = far * lax.axis_size("near")
+    owners = far * lax.axis_size("top") * lax.axis_size("low")
     tokens = hidden.shape[0]
     group_blocks = block_adapter.shape[0]
     width = tokens // group_blocks
@@ -240,7 +225,9 @@
     )
     model, query = hidden.shape[1], attended.shape[1]
     ends = [lanes, lanes + model, lanes + model + query, lanes + model + 2 * query]
-    near, mps = lax.axis_size("near"), lax.axis_size("mp")
+    lows, mps = lax.axis_size("low"), lax.axis_size("mp")
+    near = lax.axis_size("top") * lows
+    each = lax.axis_size("top") // mps
     depth = model * mps // far
     depth_out = query * mps // far
     high, wide = query_projection_weight.shape
@@ -267,15 +254,15 @@
             (far * tokens, wide_out),
         ),
         (
-            slots[1:],
-            (high, wide),
-            (high_out, wide_out),
-            (tokens, depth),
-            (tokens, depth_out),
-            (tokens, wide),
-            (tokens, wide_out),
-        ),
-        2 * near + 4 * far + owners,
+            (1, *slots[1:]),
+            (1, high, wide),
+            (1, high_out, wide_out),
+            (each, tokens, lows * high),
+            (each, tokens, lows * high_out),
+            (1, tokens, wide),
+            (1, tokens, wide_out),
+        ),
+        2 * near + 2 * far * mps * each + 2 * far + owners,
         0,
     )
     received = received.reshape(sent.shape)
@@ -341,13 +328,13 @@
             (mps * tokens, query),
         ),
         (
-            slots[1:],
-            (tokens, wide),
-            (tokens, wide_out),
-            (tokens, depth),
-            (tokens, depth_out),
-        ),
-        4 * far + owners,
+            (1, *slots[1:]),
+            (1, tokens, wide),
+            (1, tokens, wide_out),
+            (each, tokens, lows * high),
+            (each, tokens, lows * high_out),
+        ),
+        2 * far + 2 * far * mps * each + owners,
         1,
     )
     returned = returned.reshape(lifted.shape)
@@ -373,14 +360,24 @@
 
 
 def solution(mesh):
-    count = mesh.shape["dp"]
-    far = 1
-    while far * far < count or count % far or far % mesh.shape["mp"]:
-        far += 1
-    split = Mesh(
-        mesh.devices.reshape(far, count // far, mesh.shape["mp"]), ("far", "near", "mp")
-    )
-    dp = ("far", "near")
+    count, mps = mesh.shape["dp"], mesh.shape["mp"]
+
+    def on_split(*arrays):
+        low = 1
+        while arrays[4].shape[0] // count * low % 128:
+            low += 1
+        top = 1
+        while top * top * low < count // low or count % (top * low) or top % mps:
+            top += 1
+        return build(mesh, top, low)(*arrays)
+
+    return on_split
+
+
+def build(mesh, top, low):
+    shape = (top, mesh.shape["dp"] // (top * low), low, mesh.shape["mp"])
+    split = Mesh(mesh.devices.reshape(shape), ("top", "far", "low", "mp"))
+    dp = ("top", "far", "low")
     rows, factors = P(dp, "mp"), P(dp, None, "mp")
     return jax.shard_map(
         on_device,

time: 434 us -> 398 us (0.917)
  the two profiles are of different devices: /device:TPU:14 before, /device:TPU:0 now
where the time goes in v3:
time: 398 us
  Pallas kernels  340 us (85%)
  matrix products  41.3 us (10%)
  other arithmetic  7.55 us (2%)
  local copies, waits for them, and re-layouts  4.49 us (1%)
    pallas_call x2, Pallas kernels, transfer(): pl.pallas_call(kernel, out_shape=[jax.ShapeDtypeStruct(shape, jnp.bfloat1...  340 us
    dot_general x30, matrix products, product(): lax.dot_general(left, right, ((contract[:1], contract[1:]), ((), ())), pr...  41.3 us

profile of v3, /device:TPU:0, one launch (start us, length us, event | category | flops | bytes accessed | tf_op | source)
XLA Modules:
  0.0 397.9 jit_solution(11318634131437005769)
XLA Ops:
  0.7 1.3 copy-done
  2.0 0.7 and_select_fusion.1
  2.7 0.2 convert_reduce_fusion.4
  2.9 0.7 fusion.84
  3.6 0.1 reshape.117
  4.1 0.3 convolution_convert_fusion.8
  4.4 0.1 copy.22
  4.5 1.3 broadcast_multiply_fusion
  5.9 0.7 constant_dynamic-update-slice_fusion
  6.6 1.1 fusion.11
  7.7 1.1 fusion.10
  8.8 1.1 fusion.9
  9.9 1.1 fusion.8
  11.1 217.3 %shard_map.179 = (bf16[16,8,8320]{2,1,0:T(8,128)(2,1)}, bf16[1024,2048]{1,0:T(8,128)(2,1)}, bf16[1024,2048]{1,0:T(8,128)(2,1)}, bf16[512,1024]{1,0:T(8,128)(2,1)...) custom-call(bf16[16,8,8320]{2,1,0:T(8,128)(2,1)} %bitcast.refs_0_, ...), custom_call_target="tpu_custom_call" | custom-call | tf_op jit(solution)/shard_map/pallas_call | solution.py:125
  228.4 1.1 fusion.44
  229.4 2.0 fusion.27
  231.4 1.7 fusion.26
  233.1 1.8 fusion.25
  234.9 1.8 fusion.24
  236.8 3.4 psum.7
  240.2 0.3 fusion.19
  240.5 0.3 fusion.18
  240.8 0.3 fusion.17
  241.1 0.3 fusion.16
  241.4 0.3 fusion
  241.8 0.3 fusion.1
  242.1 0.3 fusion.2
  242.4 0.3 copy-done.10
  242.7 0.3 fusion.3
  243.1 1.5 maximum_bitcast_fusion.refs_0_
  244.6 1.6 copy-done.16
  246.1 3.3 convolution_convert_fusion.7.refs_3_
  249.5 3.7 convolution_convert_fusion.1.refs_1_
  253.2 3.4 convolution_convert_fusion.6.refs_4_
  256.5 3.7 convolution_convert_fusion.refs_2_
  260.2 123.0 %shard_map.180 = (bf16[16,8,8192]{2,1,0:T(8,128)(2,1)}, bf16[512,2048]{1,0:T(8,128)(2,1)}, bf16[512,2048]{1,0:T(8,128)(2,1)}, bf16[256,2048]{1,0:T(8,128)(2,1)}, bf16[256,2048]{1,0:T(8,128)(2,1)}) custom-call(bf16[16,8,8192]{2,1,0:T(8,128)(2,1)} %maximum_bitcast_fusion.refs_0_, bf16[512,2048]{1,0:T(8,128)(2,1)} %convolution_convert_fusion.1.refs_1_, ...), custom_call_target="tpu_custom_call" | custom-call | tf_op jit(solution)/shard_map/pallas_call | solution.py:125
  383.2 2.2 convert_reduce_fusion.1
  385.4 1.1 fusion.4
  386.6 0.4 convert_reduce_fusion
  387.0 1.1 fusion.5
  388.1 0.2 convert_reduce_fusion.3
  388.3 1.1 fusion.6
  389.5 0.2 convert_reduce_fusion.2
  389.7 1.1 fusion.7
  390.8 1.8 convolution_multiply_fusion.1
  392.6 1.8 convolution_multiply_fusion.3
  394.3 1.8 convolution_multiply_fusion
  396.1 1.8 convolution_multiply_fusion.2
  (49 shorter events, 0.5 us)
Async XLA Ops:
  0.6 1.4 copy-start
  0.6 7.0 %copy-start.7 = (bf16[128,2048]{1,0:T(8,128)(2,1)S(1)}, bf16[128,2048]{1,0:T(8,128)(2,1)}, u32[]{:S(2)}) copy-start(bf16[128,2048]{1,0:T(8,128)(2,1)} %refs_4_.1) | copy-start | bytes 1572868
  0.7 5.9 %copy-start.6 = (bf16[128,2048]{1,0:T(8,128)(2,1)S(1)}, bf16[128,2048]{1,0:T(8,128)(2,1)}, u32[]{:S(2)}) copy-start(bf16[128,2048]{1,0:T(8,128)(2,1)} %refs_3_.1) | copy-start | bytes 1572868
  5.9 5.2 %copy-start.1 = (bf16[128,2048]{1,0:T(8,128)(2,1)}, bf16[128,2048]{1,0:T(8,128)(2,1)S(1)}, u32[]{:S(2)}) copy-start(bf16[128,2048]{1,0:T(8,128)(2,1)S(1)} %get-tuple-element.32.refs_6_) | copy-start | bytes 1572868
  5.9 5.2 %copy-start.2 = (bf16[128,2048]{1,0:T(8,128)(2,1)}, bf16[128,2048]{1,0:T(8,128)(2,1)S(1)}, u32[]{:S(2)}) copy-start(bf16[128,2048]{1,0:T(8,128)(2,1)S(1)} %get-tuple-element.33.refs_5_) | copy-start | bytes 1572868
  228.4 4.7 %copy-start.3 = (bf16[16,8,8320]{2,1,0:T(8,128)(2,1)S(1)}, bf16[16,8,8320]{2,1,0:T(8,128)(2,1)}, u32[]{:S(2)}) copy-start(bf16[16,8,8320]{2,1,0:T(8,128)(2,1)} %get-tuple-element.20) | copy-start | bytes 6389764
  240.1 1.6 copy-start.8
  240.1 2.0 copy-start.9
  240.5 2.0 copy-start.13
  241.4 1.3 copy-start.10
  242.1 2.5 copy-start.18
  243.0 3.1 copy-start.16
  246.1 3.3 copy-start.20
  249.5 3.7 copy-start.15
  249.5 3.7 copy-start.17
  253.2 3.4 copy-start.19
  383.1 2.3 copy-start.4
  383.2 3.4 copy-start.5
  386.6 1.5 copy-start.12
  388.1 1.3 copy-start.11
  389.5 1.3 copy-start.14

commit v4 on v3

--- a/solution.py
+++ b/solution.py
@@ -79,13 +79,50 @@
     return ref.at[rows, pl.ds(pl.multiple_of(start, columns), columns)]
 
 
-def transfer(plan, arrays, out_shapes, chunks, sends, collective_id):
+def relay(place, ins, outs, groups, send_sem, recv_sem):
+    last = place.nears - 1
+
+    def within(near):
+        return jnp.logical_and(near >= 0, near <= last)
+
+    def hop(step, way, group):
+        shard = jnp.clip(place.near - way * (step - 1), 0, last)
+        target = block(outs[group], shard, ins[group].shape[0])
+        to = jnp.clip(place.near + way, 0, last)
+        at = ((step - 1) * 2 + (way > 0)) * len(groups) + groups.index(group)
+        return pltpu.make_async_remote_copy(
+            src_ref=ins[group] if step == 1 else target,
+            dst_ref=target,
+            send_sem=send_sem.at[at],
+            recv_sem=recv_sem.at[at],
+            device_id=(to // place.lows, place.far, lax.rem(to, place.lows), place.mp),
+            device_id_type=pl.DeviceIdType.MESH,
+        )
+
+    def sends(step, way):
+        ahead = within(place.near + way)
+        return jnp.logical_and(ahead, within(place.near - way * (step - 1)))
+
+    every = [(way, group) for group in groups for way in (1, -1)]
+    for step in range(1, place.nears + 1):
+        for way, group in every:
+            if step > 1:
+                arrives = within(place.near - way * (step - 1))
+                pl.when(arrives)(lambda: hop(step - 1, way, group).wait_recv())
+            if step <= last:
+                pl.when(sends(step, way))(lambda: hop(step, way, group).start())
+    for step in range(1, place.nears):
+        for way, group in every:
+            pl.when(sends(step, way))(lambda: hop(step, way, group).wait_send())
+
+
+def transfer(plan, arrays, out_shapes, chunks, sends, collective_id, relayed=(), links=0):
     count, groups = len(arrays), len(chunks)
 
     def kernel(*refs):
         ins, outs = refs[:count], refs[count : count + groups]
         held = refs[count + groups : count + 2 * groups]
-        send_sem, recv_sem, own_sem = refs[count + 2 * groups :]
+        send_sem, recv_sem, own_sem, chain_send, chain_recv = refs[count + 2 * groups :]
         place = Place()
         place.greet()
         routes = list(plan(place, ins, outs))
@@ -113,6 +150,8 @@
             copy.start()
         for inward, _ in passing:
             inward.start()
+        if relayed:
+            relay(place, ins, outs, relayed, chain_send, chain_recv)
         for inward, outward in passing:
             inward.wait()
             outward.start()
@@ -129,7 +168,8 @@
         out_specs=[anywhere] * groups,
         scratch_shapes=[pltpu.VMEM(shape, jnp.bfloat16) for shape in chunks]
         + [pltpu.SemaphoreType.DMA((sends,))] * 2
-        + [pltpu.SemaphoreType.DMA((sum(shape[0] for shape in chunks),))],
+        + [pltpu.SemaphoreType.DMA((sum(shape[0] for shape in chunks),))]
+        + [pltpu.SemaphoreType.DMA((max(links, 1),))] * 2,
         compiler_params=pltpu.CompilerParams(
             collective_id=collective_id, has_side_effects=True
         ),
@@ -143,7 +183,8 @@
     for near, device, own in place.near_peers():
         for group, weight in ((1, first), (2, second)):
             rows = weight.shape[0]
-            yield group, weight, block(outs[group], place.near, rows), device, own
+            if own:
+                yield group, weight, block(outs[group], place.near, rows), device, own
     for far, mp, at, device, own in place.feature_peers():
         for group, values in ((3, hidden), (4, attended)):
             high = outs[group].shape[1] // place.tops
@@ -264,6 +305,8 @@
         ),
         2 * near + 2 * far * mps * each + 2 * far + owners,
         0,
+        relayed=(1, 2),
+        links=4 * (near - 1),
     )
     received = received.reshape(sent.shape)
     hot, hid, att, qcot, ocot = jnp.split(received, ends, axis=1)

time: 398 us -> 347 us (0.87)
  Pallas kernels: 340 us -> 289 us
    pallas_call x2, Pallas kernels: 340 us -> 289 us  [transfer(): pl.pallas_call(kernel, out_shape=[jax.ShapeDtypeStruct(shape, jnp.bfloat1...]
where the time goes in v4:
time: 347 us
  Pallas kernels  289 us (83%)
  matrix products  41.3 us (12%)
  other arithmetic  7.55 us (2%)
  local copies, waits for them, and re-layouts  4.49 us (1%)
    pallas_call x2, Pallas kernels, transfer(): pl.pallas_call(kernel, out_shape=[jax.ShapeDtypeStruct(shape, jnp.bfloat1...  289 us
    dot_general x30, matrix products, product(): lax.dot_general(left, right, ((contract[:1], contract[1:]), ((), ())), pr...  41.3 us

profile of v4, /device:TPU:0, one launch (start us, length us, event | category | flops | bytes accessed | tf_op | source)
XLA Modules:
  0.0 346.5 jit_solution(14830946257215917569)
XLA Ops:
  0.7 1.3 copy-done
  2.0 0.7 and_select_fusion.1
  2.7 0.2 convert_reduce_fusion.4
  2.9 0.7 fusion.84
  3.6 0.1 reshape.117
  4.1 0.3 convolution_convert_fusion.8
  4.4 0.1 copy.22
  4.5 1.3 broadcast_multiply_fusion
  5.9 0.7 constant_dynamic-update-slice_fusion
  6.6 1.1 fusion.11
  7.7 1.1 fusion.10
  8.8 1.1 fusion.9
  9.9 1.1 fusion.8
  11.1 182.2 %shard_map.179 = (bf16[16,8,8320]{2,1,0:T(8,128)(2,1)}, bf16[1024,2048]{1,0:T(8,128)(2,1)}, bf16[1024,2048]{1,0:T(8,128)(2,1)}, bf16[512,1024]{1,0:T(8,128)(2,1)...) custom-call(bf16[16,8,8320]{2,1,0:T(8,128)(2,1)} %bitcast.refs_0_, ...), custom_call_target="tpu_custom_call" | custom-call | tf_op jit(solution)/shard_map/pallas_call | solution.py:164
  193.3 1.1 fusion.44
  194.4 2.0 fusion.27
  196.4 1.7 fusion.26
  198.0 1.8 fusion.25
  199.9 1.8 fusion.24
  201.7 3.4 psum.7
  205.1 0.3 fusion.19
  205.4 0.3 fusion.18
  205.7 0.3 fusion.17
  206.0 0.3 fusion.16
  206.4 0.3 fusion
  206.7 0.3 fusion.1
  207.0 0.3 fusion.2
  207.4 0.3 copy-done.10
  207.7 0.3 fusion.3
  208.0 1.5 maximum_bitcast_fusion.refs_0_
  209.5 1.6 copy-done.16
  211.1 3.3 convolution_convert_fusion.7.refs_3_
  214.4 3.7 %convolution_convert_fusion.1.refs_1_ = bf16[512,2048]{1,0:T(8,128)(2,1)} fusion(bf16[512,1024]{1,0:T(8,128)(2,1)S(1)} %copy-done.20, bf16[1024,2048]{1,0:T(8,128)(2,1)S(1)} %copy-done.16), kind=kOutput, calls=%fused_computation.3 | convolution fusion | flops 2148532224 | bytes 7340032 | tf_op jit(solution)/shard_map/dot_general | solution.py:12
  218.1 3.4 convolution_convert_fusion.6.refs_4_
  221.4 3.7 %convolution_convert_fusion.refs_2_ = bf16[512,2048]{1,0:T(8,128)(2,1)} fusion(bf16[512,1024]{1,0:T(8,128)(2,1)S(1)} %copy-done.19, bf16[1024,2048]{1,0:T(8,128)(2,1)S(1)} %copy-done.15), kind=kOutput, calls=%fused_computation.2 | convolution fusion | flops 2148532224 | bytes 7340032 | tf_op jit(solution)/shard_map/dot_general | solution.py:12
  225.1 106.7 %shard_map.180 = (bf16[16,8,8192]{2,1,0:T(8,128)(2,1)}, bf16[512,2048]{1,0:T(8,128)(2,1)}, bf16[512,2048]{1,0:T(8,128)(2,1)}, bf16[256,2048]{1,0:T(8,128)(2,1)}, bf16[256,2048]{1,0:T(8,128)(2,1)}) custom-call(bf16[16,8,8192]{2,1,0:T(8,128)(2,1)} %maximum_bitcast_fusion.refs_0_, bf16[512,2048]{1,0:T(8,128)(2,1)} %convolution_convert_fusion.1.refs_1_, ...), custom_call_target="tpu_custom_call" | custom-call | tf_op jit(solution)/shard_map/pallas_call | solution.py:164
  331.8 2.2 convert_reduce_fusion.1
  334.1 1.1 fusion.4
  335.2 0.4 convert_reduce_fusion
  335.6 1.1 fusion.5
  336.7 0.2 convert_reduce_fusion.3
  336.9 1.1 fusion.6
  338.1 0.2 convert_reduce_fusion.2
  338.3 1.1 fusion.7
  339.4 1.8 convolution_multiply_fusion.1
  341.2 1.8 convolution_multiply_fusion.3
  343.0 1.8 convolution_multiply_fusion
  344.7 1.8 convolution_multiply_fusion.2
  (49 shorter events, 0.5 us)
Async XLA Ops:
  0.6 1.4 copy-start
  0.6 7.0 %copy-start.7 = (bf16[128,2048]{1,0:T(8,128)(2,1)S(1)}, bf16[128,2048]{1,0:T(8,128)(2,1)}, u32[]{:S(2)}) copy-start(bf16[128,2048]{1,0:T(8,128)(2,1)} %refs_4_.1) | copy-start | bytes 1572868
  0.7 5.9 %copy-start.6 = (bf16[128,2048]{1,0:T(8,128)(2,1)S(1)}, bf16[128,2048]{1,0:T(8,128)(2,1)}, u32[]{:S(2)}) copy-start(bf16[128,2048]{1,0:T(8,128)(2,1)} %refs_3_.1) | copy-start | bytes 1572868
  5.9 5.2 %copy-start.1 = (bf16[128,2048]{1,0:T(8,128)(2,1)}, bf16[128,2048]{1,0:T(8,128)(2,1)S(1)}, u32[]{:S(2)}) copy-start(bf16[128,2048]{1,0:T(8,128)(2,1)S(1)} %get-tuple-element.32.refs_6_) | copy-start | bytes 1572868
  5.9 5.2 %copy-start.2 = (bf16[128,2048]{1,0:T(8,128)(2,1)}, bf16[128,2048]{1,0:T(8,128)(2,1)S(1)}, u32[]{:S(2)}) copy-start(bf16[128,2048]{1,0:T(8,128)(2,1)S(1)} %get-tuple-element.33.refs_5_) | copy-start | bytes 1572868
  193.3 4.7 %copy-start.3 = (bf16[16,8,8320]{2,1,0:T(8,128)(2,1)S(1)}, bf16[16,8,8320]{2,1,0:T(8,128)(2,1)}, u32[]{:S(2)}) copy-start(bf16[16,8,8320]{2,1,0:T(8,128)(2,1)} %get-tuple-element.20) | copy-start | bytes 6389764
  205.1 1.6 copy-start.8
  205.1 2.0 copy-start.9
  205.4 2.0 copy-start.13
  206.4 1.3 copy-start.10
  207.0 2.5 copy-start.18
  208.0 3.1 copy-start.16
  211.1 3.3 copy-start.20
  214.4 3.7 %copy-start.15 = (bf16[1024,2048]{1,0:T(8,128)(2,1)S(1)}, bf16[1024,2048]{1,0:T(8,128)(2,1)}, u32[]{:S(2)}) copy-start(bf16[1024,2048]{1,0:T(8,128)(2,1)} %get-tuple-element.24) | copy-start | bytes 12582916
  214.4 3.7 %copy-start.17 = (bf16[512,2048]{1,0:T(8,128)(2,1)S(1)}, bf16[512,2048]{1,0:T(8,128)(2,1)}, u32[]{:S(2)}) copy-start(bf16[512,2048]{1,0:T(8,128)(2,1)} %get-tuple-element.26) | copy-start | bytes 6291460
  218.1 3.4 copy-start.19
  331.8 2.3 copy-start.4
  331.8 3.4 copy-start.5
  335.2 1.5 copy-start.12
  336.7 1.3 copy-start.11
  338.1 1.3 copy-start.14
